TPU v7x, 32 devices: a whole 2x2x4 slice. The times are simulated.
32 devices in a mesh: dp: 8 (over z, y), tensor: 4 (over x, core).
Axes of the slice: x: 2, y: 2, z: 4, core: 2. Of those that a mesh axis runs over, the one named last changes fastest.
Arguments:
- tokens: bfloat16 [65536, 512], P(('dp', 'tensor')), may hold values from -6 to 6
- segment_ids: int32 [128, 512], P('dp'), may hold values from 0 to 15, never falling along the last dimension, each value on 1 to 128 neighbouring positions
- row_lengths: int32 [128], P('dp'), may hold values from 256 to 512, as said below
- qkv_weight: bfloat16 [3, 512, 512], P(None, None, 'tensor'), may hold values from -6 to 6
- qv_bias: bfloat16 [2, 512], P(None, 'tensor'), may hold values from -3 to 3
- proj_weight: bfloat16 [512, 512], P('tensor'), may hold values from -6 to 6
- proj_bias: bfloat16 [512], replicated, may hold values from -3 to 3
- first_gain: bfloat16 [512], replicated, may hold values from 0.5 to 1.5
- first_shift: bfloat16 [512], replicated, may hold values from -3 to 3
- up_weight: bfloat16 [512, 2048], P(None, 'tensor'), may hold values from -6 to 6
- up_bias: bfloat16 [2048], P('tensor'), may hold values from -3 to 3
- down_weight: bfloat16 [2048, 512], P('tensor'), may hold values from -6 to 6
- down_bias: bfloat16 [512], replicated, may hold values from -3 to 3
- second_gain: bfloat16 [512], replicated, may hold values from 0.5 to 1.5
- second_shift: bfloat16 [512], replicated, may hold values from -3 to 3
- out_grad: bfloat16 [65536, 512], P(('dp', 'tensor')), may hold values from -6 to 6
Outputs:
- layer_out: bfloat16 [65536, 512], P(('dp', 'tensor'))
- tokens_grad: float32 [65536, 512], P(('dp', 'tensor'))
- qkv_weight_grad: float32 [3, 512, 512], P(None, None, 'tensor')
- qv_bias_grad: float32 [2, 512], P(None, 'tensor')
- proj_weight_grad: float32 [512, 512], P('tensor')
- proj_bias_grad: float32 [512], replicated
- first_gain_grad: float32 [512], replicated
- first_shift_grad: float32 [512], replicated
- up_weight_grad: float32 [512, 2048], P(None, 'tensor')
- up_bias_grad: float32 [2048], P('tensor')
- down_weight_grad: float32 [2048, 512], P('tensor')
- down_bias_grad: float32 [512], replicated
- second_gain_grad: float32 [512], replicated
- second_shift_grad: float32 [512], replicated
Inputs may be any that keep to these rules, and one draw needn't show every extreme that they name: `segment_ids`: ids never fall along a packed row; every id of 0 to 15 is used by 1 to 128 consecutive tokens of each row, one example of every row holding exactly 128. `row_lengths`: of the rows of one index of dp, one of the first two holds 512 tokens and the other 256; places at or past a row's length are padding.
All inputs are finite; a program needn't handle non-finite values.
Results may differ from a plain program's by a relative error of at most 0.022.
Values may be sent and summed in bfloat16 or wider, within the bound.
A program may use at most 256 MiB of HBM per device.

v0:
```python
import jax
import jax.numpy as jnp
from jax import lax
from jax.sharding import PartitionSpec as P

HEAD_DIM = 64


levels = 127.0
norm_eps = 1e-12
masked_score = -1e30


def quantize(values, peak_value):
    step_size = peak_value / levels
    scaled = values / step_size
    return (jnp.sign(scaled) * jnp.floor(jnp.abs(scaled) + 0.5), step_size)


def passes(values):
    return jnp.sign(values) * jnp.sign(values)


def exact_gelu(values):
    return jax.nn.gelu(values, approximate=False)


def group_rows(values):
    return lax.all_gather(values, "tensor", axis=0, tiled=True)


def reduce_rows(term_fn, own_rows):
    return lax.psum_scatter(
        term_fn(jnp.int32(0), lax.axis_size("tensor") * own_rows).astype(jnp.bfloat16),
        "tensor",
        scatter_dimension=0,
        tiled=True,
    ).astype(jnp.float32)


def norm_forward(values, gain_vec, shift_vec):
    centred = values - jnp.mean(values, axis=-1, keepdims=True)
    inverse = lax.rsqrt(jnp.mean(centred * centred, axis=-1, keepdims=True) + norm_eps)
    standard = centred * inverse
    return (standard * gain_vec + shift_vec, standard, inverse)


def norm_backward(incoming, standard, inverse, gain_vec):
    scaled = incoming * gain_vec
    centred = (
        scaled
        - jnp.mean(scaled, axis=-1, keepdims=True)
        - standard * jnp.mean(scaled * standard, axis=-1, keepdims=True)
    )
    return (centred * inverse, jnp.sum(incoming * standard, axis=0), jnp.sum(incoming, axis=0))


def allowed_mask(segments, lengths, seq_len):
    places = jnp.arange(seq_len)
    same_doc = segments[:, :, None] == segments[:, None, :]
    inside = places[None, None, :] < lengths[:, None, None]
    diagonal = places[:, None] == places[None, :]
    return same_doc & inside | diagonal[None]


def pair_scores(queries, keys_low, segments, lengths):
    scale_factor = queries.shape[-1] ** (-0.5)
    scores = (
        jnp.einsum("rqhe,rkhe->rhqk", queries, keys_low, preferred_element_type=jnp.float32)
        * scale_factor
    )
    allowed = allowed_mask(segments, lengths, queries.shape[1])
    return (jnp.where(allowed[:, None], scores, masked_score), scale_factor)


def attend_pair(pieces):
    queries, keys_low, values_low, segments, lengths = pieces
    scores, scale_factor = pair_scores(queries, keys_low, segments, lengths)
    top_score = jnp.max(scores, axis=-1, keepdims=True)
    weights = jnp.exp(scores - top_score)
    totals = jnp.sum(weights, axis=-1, keepdims=True)
    attn_probs = (weights / totals).astype(jnp.bfloat16)
    context = jnp.einsum(
        "rhqk,rkhe->rqhe", attn_probs, values_low, preferred_element_type=jnp.float32
    )
    return (context, top_score + jnp.log(totals))


def attend_back(pieces):
    queries, keys_low, values_low, segments, lengths, log_total, grad_context = pieces
    scores, scale_factor = pair_scores(queries, keys_low, segments, lengths)
    attn_probs = jnp.exp(scores - log_total)
    grad_values = jnp.einsum(
        "rhqk,rqhe->rkhe",
        attn_probs.astype(jnp.bfloat16),
        grad_context,
        preferred_element_type=jnp.float32,
    )
    grad_probs = jnp.einsum(
        "rqhe,rkhe->rhqk", grad_context, values_low, preferred_element_type=jnp.float32
    )
    centre = jnp.sum(grad_probs * attn_probs, axis=-1, keepdims=True)
    grad_scores = (attn_probs * (grad_probs - centre) * scale_factor).astype(jnp.bfloat16)
    grad_queries = jnp.einsum(
        "rhqk,rkhe->rqhe", grad_scores, keys_low, preferred_element_type=jnp.float32
    )
    grad_keys = jnp.einsum(
        "rhqk,rqhe->rkhe", grad_scores, queries, preferred_element_type=jnp.float32
    )
    return (grad_queries, grad_keys, grad_values)


def local(
    tokens,
    segment_ids,
    row_lengths,
    qkv_weight,
    qv_bias,
    proj_weight,
    proj_bias,
    first_gain,
    first_shift,
    up_weight,
    up_bias,
    down_weight,
    down_bias,
    second_gain,
    second_shift,
    out_grad,
):
    own_rows = tokens.shape[0]
    rows_here = segment_ids.shape[0]
    seq_len = segment_ids.shape[1]
    heads_here = qkv_weight.shape[2] // HEAD_DIM
    token_vals = tokens.astype(jnp.float32)
    qkv_vals = qkv_weight.astype(jnp.float32)
    proj_vals = proj_weight.astype(jnp.float32)
    up_vals = up_weight.astype(jnp.float32)
    down_vals = down_weight.astype(jnp.float32)
    top_qkv = jnp.max(jnp.abs(qkv_vals), axis=(1, 2))
    top_proj = jnp.max(jnp.abs(proj_vals))
    top_up = jnp.max(jnp.abs(up_vals))
    top_down = jnp.max(jnp.abs(down_vals))
    peak_qkv, peak_proj, peak_up, peak_down = lax.pmax(
        (top_qkv, top_proj, top_up, top_down), "tensor"
    )
    peak_tokens = lax.pmax(jnp.max(jnp.abs(token_vals)), ("dp", "tensor"))
    token_ints, step_tokens = quantize(token_vals, peak_tokens)
    qkv_ints, step_qkv = quantize(qkv_vals, peak_qkv[:, None, None])
    proj_ints, step_proj = quantize(proj_vals, peak_proj)
    up_ints, step_up = quantize(up_vals, peak_up)
    down_ints, step_down = quantize(down_vals, peak_down)
    qkv_low = qkv_ints.astype(jnp.bfloat16)
    proj_low = proj_ints.astype(jnp.bfloat16)
    up_low = up_ints.astype(jnp.bfloat16)
    down_low = down_ints.astype(jnp.bfloat16)
    group_tokens = group_rows(token_ints.astype(jnp.bfloat16))
    total_rows = group_tokens.shape[0]
    qkv_raw = jnp.einsum("td,idh->ith", group_tokens, qkv_low, preferred_element_type=jnp.float32)
    qkv_out = qkv_raw * (step_tokens * step_qkv)
    bias_vals = qv_bias.astype(jnp.float32)
    pair_shape = (rows_here // 2, 2, seq_len, heads_here, HEAD_DIM)
    queries = (qkv_out[0] + bias_vals[0]).astype(jnp.bfloat16).reshape(pair_shape)
    keys_low = qkv_out[1].astype(jnp.bfloat16).reshape(pair_shape)
    values_low = (qkv_out[2] + bias_vals[1]).astype(jnp.bfloat16).reshape(pair_shape)
    pair_segments = segment_ids.reshape(rows_here // 2, 2, seq_len)
    pair_lengths = row_lengths.reshape(rows_here // 2, 2)
    context_pairs, log_totals = lax.map(
        attend_pair, (queries, keys_low, values_low, pair_segments, pair_lengths)
    )
    context_low = context_pairs.reshape(total_rows, heads_here * HEAD_DIM).astype(jnp.bfloat16)

    def proj_term(row_start, row_count):
        return jnp.dot(context_low, proj_low, preferred_element_type=jnp.float32)

    proj_raw = reduce_rows(proj_term, own_rows)
    first_in = token_vals + (proj_raw * step_proj + proj_bias.astype(jnp.float32))
    first_gain_vals = first_gain.astype(jnp.float32)
    normed, first_standard, first_inverse = norm_forward(
        first_in, first_gain_vals, first_shift.astype(jnp.float32)
    )
    normed_low = normed.astype(jnp.bfloat16)
    up_full, up_bias_full, down_full = (
        lax.all_gather(up_low, "tensor", axis=1, tiled=True),
        lax.all_gather(up_bias, "tensor", axis=0, tiled=True),
        lax.all_gather(down_low, "tensor", axis=0, tiled=True),
    )
    pre_act = jnp.dot(
        normed_low, up_full, preferred_element_type=jnp.float32
    ) * step_up + up_bias_full.astype(jnp.float32)
    activated, gelu_pull = jax.vjp(exact_gelu, pre_act)
    act_low = activated.astype(jnp.bfloat16)
    down_raw = jnp.dot(act_low, down_full, preferred_element_type=jnp.float32)
    second_in = normed + (down_raw * step_down + down_bias.astype(jnp.float32))
    second_gain_vals = second_gain.astype(jnp.float32)
    layer_out, second_standard, second_inverse = norm_forward(
        second_in, second_gain_vals, second_shift.astype(jnp.float32)
    )
    grad_second, second_gain_grad, second_shift_grad = norm_backward(
        out_grad.astype(jnp.float32), second_standard, second_inverse, second_gain_vals
    )
    down_bias_grad = jnp.sum(grad_second, axis=0)
    grad_down = (grad_second * step_down).astype(jnp.bfloat16)
    down_full_grad = jnp.einsum("tf,td->fd", act_low, grad_down, preferred_element_type=jnp.float32)
    act_grad = jnp.einsum("td,fd->tf", grad_down, down_full, preferred_element_type=jnp.float32)
    (pre_grad,) = gelu_pull(act_grad)
    up_bias_full_grad = jnp.sum(pre_grad, axis=0)
    grad_up = (pre_grad * step_up).astype(jnp.bfloat16)
    up_full_grad = jnp.einsum("td,tf->df", normed_low, grad_up, preferred_element_type=jnp.float32)
    normed_back = jnp.einsum("tf,df->td", grad_up, up_full, preferred_element_type=jnp.float32)
    up_int_grad, up_bias_grad, down_int_grad = (
        lax.psum_scatter(
            up_full_grad.astype(jnp.bfloat16), "tensor", scatter_dimension=1, tiled=True
        ).astype(jnp.float32),
        lax.psum_scatter(
            up_bias_full_grad.astype(jnp.bfloat16), "tensor", scatter_dimension=0, tiled=True
        ).astype(jnp.float32),
        lax.psum_scatter(
            down_full_grad.astype(jnp.bfloat16), "tensor", scatter_dimension=0, tiled=True
        ).astype(jnp.float32),
    )
    grad_normed = grad_second + normed_back
    grad_first, first_gain_grad, first_shift_grad = norm_backward(
        grad_normed, first_standard, first_inverse, first_gain_vals
    )
    proj_bias_grad = jnp.sum(grad_first, axis=0)
    grad_proj = (grad_first * step_proj).astype(jnp.bfloat16)
    group_grad = group_rows(grad_proj)
    proj_int_grad = jnp.einsum(
        "tc,td->cd", context_low, group_grad, preferred_element_type=jnp.float32
    )
    grad_context = jnp.einsum(
        "td,cd->tc", group_grad, proj_low, preferred_element_type=jnp.float32
    ).astype(jnp.bfloat16)
    grad_pairs = lax.map(
        attend_back,
        (
            queries,
            keys_low,
            values_low,
            pair_segments,
            pair_lengths,
            log_totals,
            grad_context.reshape(pair_shape),
        ),
    )
    grad_queries = grad_pairs[0].reshape(total_rows, heads_here * HEAD_DIM)
    grad_keys = grad_pairs[1].reshape(total_rows, heads_here * HEAD_DIM)
    grad_values = grad_pairs[2].reshape(total_rows, heads_here * HEAD_DIM)
    qv_bias_grad = jnp.stack([jnp.sum(grad_queries, axis=0), jnp.sum(grad_values, axis=0)])
    grad_qkv = (
        jnp.stack([grad_queries, grad_keys, grad_values]) * (step_tokens * step_qkv)
    ).astype(jnp.bfloat16)
    qkv_int_grad = jnp.einsum(
        "td,ith->idh", group_tokens, grad_qkv, preferred_element_type=jnp.float32
    )

    def input_term(row_start, row_count):
        return jnp.einsum("ith,idh->td", grad_qkv, qkv_low, preferred_element_type=jnp.float32)

    token_int_grad = reduce_rows(input_term, own_rows)
    tokens_grad = grad_first + token_int_grad * passes(token_vals) / step_tokens
    shard_sums = (
        lax.psum(qkv_int_grad.astype(jnp.bfloat16), "dp").astype(jnp.float32),
        lax.psum(qv_bias_grad.astype(jnp.bfloat16), "dp").astype(jnp.float32),
        lax.psum(proj_int_grad.astype(jnp.bfloat16), "dp").astype(jnp.float32),
        lax.psum(up_int_grad.astype(jnp.bfloat16), "dp").astype(jnp.float32),
        lax.psum(up_bias_grad.astype(jnp.bfloat16), "dp").astype(jnp.float32),
        lax.psum(down_int_grad.astype(jnp.bfloat16), "dp").astype(jnp.float32),
    )
    common_sums = lax.psum(
        (
            proj_bias_grad,
            first_gain_grad,
            first_shift_grad,
            down_bias_grad,
            second_gain_grad,
            second_shift_grad,
        ),
        ("dp", "tensor"),
    )
    return (
        layer_out.astype(jnp.bfloat16),
        tokens_grad,
        shard_sums[0] * passes(qkv_vals) / step_qkv,
        shard_sums[1],
        shard_sums[2] * passes(proj_vals) / step_proj,
        common_sums[0],
        common_sums[1],
        common_sums[2],
        shard_sums[3] * passes(up_vals) / step_up,
        shard_sums[4],
        shard_sums[5] * passes(down_vals) / step_down,
        common_sums[3],
        common_sums[4],
        common_sums[5],
    )


def solution(mesh):
    in_specs = (
        P(("dp", "tensor"), None),
        P("dp", None),
        P("dp"),
        P(None, None, "tensor"),
        P(None, "tensor"),
        P("tensor", None),
        P(),
        P(),
        P(),
        P(None, "tensor"),
        P("tensor"),
        P("tensor", None),
        P(),
        P(),
        P(),
        P(("dp", "tensor"), None),
    )
    out_specs = (
        P(("dp", "tensor"), None),
        P(("dp", "tensor"), None),
        P(None, None, "tensor"),
        P(None, "tensor"),
        P("tensor", None),
        P(),
        P(),
        P(),
        P(None, "tensor"),
        P("tensor"),
        P("tensor", None),
        P(),
        P(),
        P(),
    )
    return jax.shard_map(local, mesh=mesh, in_specs=in_specs, out_specs=out_specs, check_vma=False)
```

profile of v0, /device:TPU:0, one launch (start us, length us, event | category | flops | bytes accessed | tf_op | source)
XLA Modules:
  0.0 994.6 jit_solution(8438317445170648339)
XLA Ops:
  9.8 42.2 %pmax.36 = f32[]{:T(128)} all-reduce(f32[]{:T(128)} %fusion.88), channel_id=1, replica_groups=mesh['dp'=8,'tensor'=4] {'dp','tensor'}, use_global_device_ids=true, to_apply=%region_3.0 | all-reduce | flops 1 | bytes 8 | tf_op jit(solution)/shard_map/pmax | solution.py:147
  52.6 4.8 multiply_convert_fusion.5
  59.2 7.0 all-reduce.2
  69.9 46.0 %all-gather.6.cloned.1.call-done = bf16[8192,512]{1,0:T(8,128)(2,1)} async-done(((bf16[2048,512]{1,0:T(8,128)(2,1)}), bf16[8192,512]{1,0:T(8,128)(2,1)}) %all-gather.6.cloned.1.call-update) | async-done | bytes 8388624 | tf_op jit(solution)/shard_map/all_gather | solution.py:29
  115.9 6.2 multiply_bitcast_fusion
  122.1 3.9 fusion.132
  127.6 6.6 squeeze.37
  134.2 6.6 squeeze.38
  140.7 4.5 convert_element_type.171
  145.2 4.2 copy.68
  156.7 59.9 %while.28 = (s32[]{:T(128)}, bf16[8,2,512,2,64]{2,4,3,1,0:T(8,128)(2,1)S(1)}, f32[8,2,2,512,1]{3,2,1,4,0:T(2,128)}, bf16[8,2,512,2,64]{2,4,3,1,0:T(8,128)(2,1)},...) while((s32[]{:T(128)}, ...), condition=%wide.region_7.0_spmd.clone, body=%wide.region_4.7_spmd.sunk.clone | while | flops 282852352 | bytes 16597121 | solution.py:168
  223.4 5.7 convolution_convert_fusion
  233.3 5.2 all-gather
  238.6 62.4 %reduce-scatter.5.cloned.1.call-done = bf16[2048,512]{1,0:T(8,128)(2,1)} async-done(((bf16[8192,512]{1,0:T(8,128)(2,1)}), bf16[2048,512]{1,0:T(8,128)(2,1)}) %reduce-scatter.5.cloned.1.call-update) | async-done | bytes 2097168 | tf_op jit(solution)/shard_map/reduce_scatter | solution.py:33
  305.0 20.9 %all-gather.8.cloned.1.call-done = bf16[512,2048]{1,0:T(8,128)(2,1)} async-done(((bf16[512,512]{1,0:T(8,128)(2,1)}), bf16[512,2048]{1,0:T(8,128)(2,1)}) %all-gather.8.cloned.1.call-update) | async-done | bytes 2097168 | tf_op jit(solution)/shard_map/all_gather | solution.py:184
  325.9 45.8 %multiply_convert_fusion.2 = (bf16[2048,2048]{1,0:T(8,128)(2,1)}, f32[2048,2048]{1,0:T(8,128)}, f32[2048,2048]{1,0:T(8,128)}) fusion(f32[2048]{0:T(1024)S(1)} %bitcast.166, f32[]{:T(128)S(6)} %div.112, bf16[512,2048]{1,0:T(8,128)(2,1)} %all-gather.8.cloned.1.call-done, f32[512]{0:T(512)S(1)} %convert_element_type.180, f32[512]{0:T(512)S(1)} %convert_element_type.179, ...), kind=kOutput, calls=%fused_computation.79 | convolution fusion | flops 4586471424 | bytes 48265224 | tf_op jit(solution)/shard_map/dot_general | solution.py:188
  371.6 9.0 fusion.133
  385.1 4.9 fusion.128
  390.0 22.6 %fusion.134 = (bf16[2048]{0:T(1024)(128)(2,1)S(1)}, f32[2048,2048]{1,0:T(8,128)}) fusion(f32[2048,2048]{1,0:T(8,128)} %get-tuple-element.289, bf16[2048,512]{1,0:T(8,128)(2,1)} %all-gather.10.cloned.1.call-done, f32[2048,512]{1,0:T(8,128)} %get-tuple-element.285, f32[]{:T(128)S(6)} %div.115, f32[2048]{0:T(1024)S(1)} %bitcast.167, ...), kind=kOutput, calls=%fused_computation.200 | convolution fusion | flops 4364171264 | bytes 56635400 | tf_op jit(solution)/shard_map/td,fd->tf/dot_general | solution.py:205
  412.6 11.7 %multiply_reduce_fusion.1 = (f32[512]{0:T(512)S(1)}, f32[2048]{0:T(1024)S(1)}, f32[2048]{0:T(1024)S(1)}, f32[512]{0:T(512)S(1)}, f32[2048,512]{1,0:T(8,128)S(1)}) fusion(f32[2048]{0:T(1024)S(1)} %add_rsqrt_fusion.1, f32[2048]{0:T(1024)S(1)} %broadcast_multiply_fusion.5, f32[512]{0:T(512)S(1)} %convert_element_type.178, f32[]{:T(128)S(6)} %div.107, ...), kind=kOutput, calls=%fused_computation.126 | convolution fusion | flops 4319079424 | bytes 31498248 | tf_op jit(solution)/shard_map/tf,df->td/dot_general | solution.py:210
  430.7 13.4 %fusion.99 = bf16[512,2048]{1,0:T(8,128)(2,1)} fusion(f32[2048,2048]{1,0:T(8,128)} %get-tuple-element.302, f32[]{:T(128)S(6)} %div.112, f32[512]{0:T(512)S(1)} %convert_element_type.180, f32[512]{0:T(512)S(1)} %convert_element_type.179, bf16[2048,512]{1,0:T(8,128)(2,1)} %reduce-scatter.5.cloned.1.call-done, bf16[2048,512]{1,0:T(8,128)(2,1)S(1)} %copy-done, ...), kind=kOutput, calls=%fused_computation.145 | convolution fusion | flops 4314890240 | bytes 23091208 | tf_op jit(solution)/shard_map/td,tf->df/dot_general | solution.py:209
  444.2 10.5 %convolution_convert_fusion.2 = bf16[2048,512]{1,0:T(8,128)(2,1)} fusion(bf16[2048,2048]{1,0:T(8,128)(2,1)} %get-tuple-element.288, f32[2048,512]{1,0:T(8,128)} %get-tuple-element.285, f32[]{:T(128)S(6)} %div.115), kind=kOutput, calls=%fused_computation.144 | convolution fusion | flops 4298113024 | bytes 14680068 | tf_op jit(solution)/shard_map/tf,td->fd/dot_general | solution.py:204
  454.8 34.2 %all-gather.12.cloned.1.call-done = bf16[8192,512]{1,0:T(8,128)(2,1)} async-done(((bf16[2048,512]{1,0:T(8,128)(2,1)}), bf16[8192,512]{1,0:T(8,128)(2,1)}) %all-gather.12.cloned.1.call-update) | async-done | bytes 8388624 | tf_op jit(solution)/shard_map/all_gather | solution.py:29
  489.0 7.1 convolution_convert_fusion.1
  496.1 8.5 reshape.233
  504.6 10.6 %copy.72 = bf16[8,2,512,2,64]{2,4,3,1,0:T(8,128)(2,1)} copy(bf16[8,2,512,2,64]{4,3,2,1,0:T(2,128)(2,1)} %reshape.233) | data formatting | bytes 4194304 | tf_op jit(solution)/shard_map/while | solution.py:235
  515.2 250.8 %while.29 = (s32[]{:T(128)}, f32[8,2,512,2,64]{2,4,3,1,0:T(8,128)}, f32[8,2,512,2,64]{2,1,0,4,3:T(2,128)}, f32[8,2,512,2,64]{2,4,3,1,0:T(8,128)}, bf16[8,2,512,2...) while((s32[]{:T(128)}, f32[8,2,512,2,64]{2,4,3,1,0:T(8,128)}, ...), condition=%wide.region_25.26_spmd.clone, body=%wide.region_23.25_spmd.sunk.clone | while | flops 687609856 | bytes 52209824 | solution.py:235
  518.0 4.4 subtract_exponential_fusion.4
  526.2 8.4 fusion.202
  534.6 7.2 fusion.203
  549.8 4.4 subtract_exponential_fusion.4
  558.0 8.1 fusion.202
  566.1 7.1 fusion.203
  581.2 4.4 subtract_exponential_fusion.4
  589.4 8.0 fusion.202
  597.4 7.1 fusion.203
  612.4 4.4 subtract_exponential_fusion.4
  620.6 8.0 fusion.202
  628.6 7.1 fusion.203
  643.7 4.4 subtract_exponential_fusion.4
  651.9 8.1 fusion.202
  659.9 7.1 fusion.203
  675.0 4.4 subtract_exponential_fusion.4
  683.2 8.1 fusion.202
  691.2 7.1 fusion.203
  706.3 4.4 subtract_exponential_fusion.4
  714.4 8.0 fusion.202
  722.5 7.1 fusion.203
  737.5 4.4 subtract_exponential_fusion.4
  745.7 8.0 fusion.202
  753.7 7.1 fusion.203
  766.0 7.4 copy.75
  773.4 6.6 stack_reshape.11
  780.0 7.0 stack_reshape.10
  787.0 7.3 copy.73
  794.3 6.6 stack_reshape.9
  801.0 6.1 convolution_convert_fusion.3
  808.7 7.6 fusion.104
  816.4 10.2 %bitcast_convert_fusion = bf16[8192,512]{1,0:T(8,128)(2,1)} fusion(bf16[3,512,128]{1,2,0:T(8,128)(2,1)S(1)} %copy-done.9, f32[3]{0:T(128)S(1)} %copy-done.23, f32[1,8192,128]{1,2,0:T(8,128)} %stack_reshape.11, f32[1,8192,128]{1,2,0:T(8,128)} %stack_reshape.10, f32[1,8192,128]{1,2,0:T(8,128)} %stack_reshape.9, f32[3]{0:T(128)S(1)} %copy-done.27), kind=kOutput, calls=%fused_computation.76 | convolution fusion | flops 3239575552 | bytes 21364760 | tf_op jit(solution)/shard_map/ith,idh->td/dot_general | solution.py:259
  828.6 6.6 all-reduce
  835.2 40.8 %all-reduce.1 = (f32[512]{0:T(512)}, f32[512]{0:T(512)}, f32[512]{0:T(512)}, f32[512]{0:T(512)}, f32[512]{0:T(512)}, /*index=5*/f32[512]{0:T(512)}) all-reduce(f32[512]{0:T(512)S(1)} %get-tuple-element.286, f32[512]{0:T(512)S(1)} %get-tuple-element.220, ...), channel_id=1, replica_groups=mesh['dp'=8,'tensor'=4] {'dp','tensor'}, use_global_device_ids=true, to_apply=%region_33.34 | all-reduce | flops 3072 | bytes 24576 | tf_op jit(solution)/shard_map/psum | solution.py:271
  882.5 22.1 %all-reduce.3 = (bf16[2,128]{1,0:T(2,128)(2,1)}, bf16[512]{0:T(512)(128)(2,1)S(1)}) all-reduce(bf16[2,128]{1,0:T(2,128)(2,1)S(1)} %pad_maximum_fusion, bf16[512]{0:T(512)(128)(2,1)S(1)} %dynamic-slice.1), channel_id=1, replica_groups=mesh['dp'=8,'tensor'=4] {'dp'}, use_global_device_ids=true, to_apply=%region_30.31 | all-reduce | flops 768 | bytes 3072 | tf_op jit(solution)/shard_map/psum | solution.py:265
  918.3 62.9 %reduce-scatter.7.cloned.1.call-done = bf16[2048,512]{1,0:T(8,128)(2,1)} async-done(((bf16[8192,512]{1,0:T(8,128)(2,1)}), bf16[2048,512]{1,0:T(8,128)(2,1)}) %reduce-scatter.7.cloned.1.call-update) | async-done | bytes 2097168 | tf_op jit(solution)/shard_map/reduce_scatter | solution.py:33
  981.2 6.6 fusion.92
  (308 shorter events, 215.8 us)
Async XLA Ops:
  7.2 50.3 %copy-start.20 = (bf16[3,512,128]{2,1,0:T(8,128)(2,1)S(1)}, bf16[3,512,128]{2,1,0:T(8,128)(2,1)}, u32[]{:S(2)}) copy-start(bf16[3,512,128]{2,1,0:T(8,128)(2,1)} %param.23) | copy-start | bytes 1179652
  7.2 50.5 %copy-start.17 = (bf16[128,512]{1,0:T(8,128)(2,1)S(1)}, bf16[128,512]{1,0:T(8,128)(2,1)}, u32[]{:S(2)}) copy-start(bf16[128,512]{1,0:T(8,128)(2,1)} %param.25) | copy-start | bytes 393220
  7.2 108.7 %all-gather.6.cloned.1.call-start = ((), (), s32[]{:S(2)}) async-start(), calls=%async_computation.4 | async-start | bytes 10485760 | tf_op jit(solution)/shard_map/all_gather | solution.py:29
  9.8 48.7 %copy-start.10 = (bf16[512,512]{1,0:T(8,128)(2,1)S(1)}, bf16[512,512]{1,0:T(8,128)(2,1)}, u32[]{:S(2)}) copy-start(bf16[512,512]{1,0:T(8,128)(2,1)} %param.29) | copy-start | bytes 1572868
  9.8 48.7 %copy-start.12 = (bf16[512,512]{1,0:T(8,128)(2,1)S(1)}, bf16[512,512]{1,0:T(8,128)(2,1)}, u32[]{:S(2)}) copy-start(bf16[512,512]{1,0:T(8,128)(2,1)} %param.31) | copy-start | bytes 1572868
  52.6 14.2 %copy-start.39 = (bf16[2,128]{1,0:T(2,128)(2,1)S(1)}, bf16[2,128]{1,0:T(2,128)(2,1)}, u32[]{:S(2)}) copy-start(bf16[2,128]{1,0:T(2,128)(2,1)} %param.24) | copy-start | bytes 1540
  52.6 14.3 %copy-start.21 = (s32[16,512]{1,0:T(8,128)S(1)}, s32[16,512]{1,0:T(8,128)}, u32[]{:S(2)}) copy-start(s32[16,512]{1,0:T(8,128)} %param.21) | copy-start | bytes 98308
  52.6 14.9 %copy-start.38 = (s32[16]{0:T(128)S(1)}, s32[16]{0:T(128)}, u32[]{:S(2)}) copy-start(s32[16]{0:T(128)} %param.22) | copy-start | bytes 196
  57.4 243.6 %reduce-scatter.5.cloned.1.call-start = ((), (), s32[]{:S(2)}) async-start(), calls=%async_computation.5 | async-start | bytes 10485760 | tf_op jit(solution)/shard_map/reduce_scatter | solution.py:33
  57.7 64.4 %copy-start.8 = (bf16[3,512,128]{1,2,0:T(8,128)(2,1)}, bf16[3,512,128]{1,2,0:T(8,128)(2,1)S(1)}, u32[]{:S(2)}) copy-start(bf16[3,512,128]{1,2,0:T(8,128)(2,1)S(1)} %copy.65) | copy-start | bytes 1179652
  69.9 52.2 %copy-start.22 = (f32[3]{0:T(128)}, f32[3]{0:T(128)S(1)}, u32[]{:S(2)}) copy-start(f32[3]{0:T(128)S(1)} %get-tuple-element.295) | copy-start | bytes 40
  69.9 52.2 %copy-start.26 = (f32[3]{0:T(128)}, f32[3]{0:T(128)S(1)}, u32[]{:S(2)}) copy-start(f32[3]{0:T(128)S(1)} %get-tuple-element.296) | copy-start | bytes 40
  145.2 4.2 copy-start.5
  149.5 3.6 copy-start.6
  149.5 3.6 copy-start.37
  216.5 6.8 copy-start.29
  216.5 6.8 copy-start.18
  223.4 5.7 copy-start.2
  229.0 4.2 copy-start.30
  229.0 4.3 copy-start.31
  229.1 9.5 copy-start.32
  229.1 9.5 copy-start.33
  229.1 9.5 copy-start.34
  229.1 9.5 copy-start.35
  229.1 9.5 copy-start.36
  229.1 71.9 %copy-start = (bf16[2048,512]{1,0:T(8,128)(2,1)S(1)}, bf16[2048,512]{1,0:T(8,128)(2,1)}, u32[]{:S(2)}) copy-start(bf16[2048,512]{1,0:T(8,128)(2,1)} %param.20) | copy-start | bytes 6291460
  229.1 96.7 %all-gather.8.cloned.1.call-start = ((), (), s32[]{:S(2)}) async-start(), calls=%async_computation.6 | async-start | bytes 2621440 | tf_op jit(solution)/shard_map/all_gather | solution.py:184
  231.3 140.4 %all-gather.10.cloned.1.call-start = ((), (), s32[]{:S(2)}) async-start(), calls=%async_computation.7 | async-start | bytes 2621440 | tf_op jit(solution)/shard_map/all_gather | solution.py:186
  233.2 255.7 %all-gather.12.cloned.1.call-start = ((), (), s32[]{:S(2)}) async-start(), calls=%async_computation.8 | async-start | bytes 10485760 | tf_op jit(solution)/shard_map/all_gather | solution.py:29
  301.0 2.6 copy-start.3
  380.6 1.6 copy-start.7
  412.6 11.7 %copy-start.4 = (bf16[2048,512]{1,0:T(8,128)(2,1)S(1)}, bf16[2048,512]{1,0:T(8,128)(2,1)}, u32[]{:S(2)}) copy-start(bf16[2048,512]{1,0:T(8,128)(2,1)} %reduce-scatter.5.cloned.1.call-done) | copy-start | bytes 6291460
  426.6 2.0 copy-start.1
  430.5 385.8 %reduce-scatter.9.cloned.1.call-start = ((), (), s32[]{:S(2)}) async-start(), calls=%async_computation.10 | async-start | bytes 2621440 | tf_op jit(solution)/shard_map/reduce_scatter | solution.py:212
  444.1 372.2 %reduce-scatter.11.cloned.1.call-start = ((), (), s32[]{:S(2)}) async-start(), calls=%async_computation.11 | async-start | bytes 2621440 | tf_op jit(solution)/shard_map/reduce_scatter | solution.py:218
  444.2 44.8 %copy-start.19 = (bf16[128,512]{1,0:T(8,128)(2,1)S(1)}, bf16[128,512]{1,0:T(8,128)(2,1)}, u32[]{:S(2)}) copy-start(bf16[128,512]{1,0:T(8,128)(2,1)} %param.25) | copy-start | bytes 393220
  454.7 452.5 %all-reduce.7.cloned.1.call-start = ((), (), s32[]{:S(2)}) async-start(), calls=%async_computation.12 | async-start | bytes 3145728 | tf_op jit(solution)/shard_map/psum | solution.py:264
  801.0 6.1 copy-start.14
  801.0 6.5 copy-start.15
  801.0 7.7 copy-start.16
  801.0 7.7 copy-start.27
  808.7 7.7 copy-start.9
  808.7 7.7 copy-start.23
  816.4 164.8 %reduce-scatter.7.cloned.1.call-start = ((), (), s32[]{:S(2)}) async-start(), calls=%async_computation.9 | async-start | bytes 10485760 | tf_op jit(solution)/shard_map/reduce_scatter | solution.py:33
  826.7 0.7 copy-start.40
  826.7 8.5 copy-start.24
  826.7 8.5 copy-start.25
  826.7 8.5 copy-start.28
  878.6 34.9 %copy-start.11 = (bf16[512,512]{1,0:T(8,128)(2,1)S(1)}, bf16[512,512]{1,0:T(8,128)(2,1)}, u32[]{:S(2)}) copy-start(bf16[512,512]{1,0:T(8,128)(2,1)} %param.29) | copy-start | bytes 1572868
  878.6 37.3 %copy-start.13 = (bf16[512,512]{1,0:T(8,128)(2,1)S(1)}, bf16[512,512]{1,0:T(8,128)(2,1)}, u32[]{:S(2)}) copy-start(bf16[512,512]{1,0:T(8,128)(2,1)} %param.31) | copy-start | bytes 1572868
Sparse Core Ops, SparseCore 0:
  57.6 58.2 all-gather.5
  229.3 71.7 reduce-scatter.4
  303.2 22.5 all-gather.7
  327.9 22.5 all-gather.9
  430.6 58.2 all-gather.11
  491.5 31.4 reduce-scatter.8
  525.5 31.4 reduce-scatter.10
  816.5 90.6 all-reduce.6
  910.0 71.1 reduce-scatter.6
where the time goes:
time: 1000 us; the launch traced here: 995 us
  matrix products  409 us (41%)
  waiting for transfers between devices  227 us (23%)
  local copies, waits for them, and re-layouts  131 us (13%)
  blocking collectives  124 us (12%)
  other arithmetic  84.1 us (8%)
  between operations  18.7 us (2%)
    reduce_scatter x2, waiting for transfers between devices, reduce_rows(): lax.psum_scatter(term_fn(jnp.int32(0), lax.axis_size('tensor') * own_rows...  125 us
    all_gather x2, waiting for transfers between devices, group_rows(): return lax.all_gather(values, 'tensor', axis=0, tiled=True)  80.2 us
    dot_general x8, matrix products, attend_back(): jnp.einsum('rhqk,rkhe->rqhe', grad_scores, keys_low, preferred_element_ty...  64.8 us
    dot_general x8, matrix products, attend_back(): jnp.einsum('rhqk,rqhe->rkhe', grad_scores, queries, preferred_element_typ...  57 us
    dot_general x16, matrix products, pair_scores(): jnp.einsum('rqhe,rkhe->rhqk', queries, keys_low, preferred_element_type=j...  51.8 us
    dot_general x1, matrix products, local(): jnp.dot(normed_low, up_full, preferred_element_type=jnp.float32) * step_up  45.8 us
    pmax x1, blocking collectives, local(): peak_tokens = lax.pmax(jnp.max(jnp.abs(token_vals)), ('dp', 'tensor'))  42.2 us
    psum x1, blocking collectives, local(): lax.psum((proj_bias_grad, first_gain_grad, first_shift_grad, down_bias_gr...  40.8 us
  transfers between devices with their start and end apart: 9, of which 6 were waited for; matrix products, arithmetic and copies ran while one was open for 44% of the time, Pallas kernels for 0%

commit v1 on v0

v1 whole, which is shorter than its diff:
```python
import jax
import jax.numpy as jnp
from jax import lax
from jax.experimental import pallas as pl
from jax.experimental.pallas import tpu as pltpu
from jax.sharding import PartitionSpec as P

D = 512
HEADS = 8
HEAD_DIM = 64
FF = 2048
SEQ = 512
PAIRS = 4
LANES = 128
LEVELS = 127.0
EPS = 1e-12
MASKED = -1e30
LOG2E = 1.4426950408889634
SCORE_SCALE = 0.125 * LOG2E
VMEM_LIMIT = 58 << 20
F32 = jnp.float32
BF16 = jnp.bfloat16
TILES = ((0, 256, 0, 384), (256, 512, 128, 512))


def rounded(scaled):
    magnitude = jnp.floor(jnp.abs(scaled) + 0.5)
    return jnp.where(scaled < 0.0, -magnitude, magnitude)


def dot_nn(a, b):
    return lax.dot_general(a, b, (((1,), (0,)), ((), ())), preferred_element_type=F32)


def dot_nt(a, b):
    return lax.dot_general(a, b, (((1,), (1,)), ((), ())), preferred_element_type=F32)


def dot_tn(a, b):
    return lax.dot_general(a, b, (((0,), (0,)), ((), ())), preferred_element_type=F32)


def head_mask(head, rows):
    lane = lax.broadcasted_iota(jnp.int32, (rows, LANES), 1)
    return (lane < HEAD_DIM) if head == 0 else (lane >= HEAD_DIM)


def both(left, right):
    return jnp.concatenate(
        [left[:, :128], left[:, 128:] + right[:, :256], right[:, 256:]], axis=1
    )


MESH = pl.DeviceIdType.MESH
GROUPS = ("core", "x", "y", "z")


def group_sizes(tensor_size, dp_size):
    return {"core": 2, "x": tensor_size // 2, "y": 2, "z": dp_size // 2}


class Place:
    def __init__(self, sizes):
        t, d = lax.axis_index("tensor"), lax.axis_index("dp")
        self.sizes = sizes
        self.part = t
        self.at = {"core": t % 2, "x": t // 2, "y": d % 2, "z": d // 2}

    def size(self, group):
        return self.sizes[group]

    def peer(self, group, k):
        at = dict(self.at)
        at[group] = (at[group] + k) % self.sizes[group]
        return at[group], (at["z"] * 2 + at["y"], at["x"] * 2 + at["core"])

    def greet(self):
        barrier = pltpu.get_barrier_semaphore()
        count = 0
        for group in GROUPS:
            for k in range(1, self.sizes[group]):
                pl.semaphore_signal(
                    barrier, inc=1, device_id=self.peer(group, k)[1], device_id_type=MESH
                )
                count += 1
        pl.semaphore_wait(barrier, count)


class Sems:
    def __init__(self, send, recv):
        self.send, self.recv = send, recv

    def copy(self, at, source, target, device):
        return pltpu.make_async_remote_copy(
            src_ref=source,
            dst_ref=target,
            send_sem=self.send.at[at],
            recv_sem=self.recv.at[at],
            device_id=device,
            device_id_type=MESH,
        )


def exchange(place, group, source, target, sems, base):
    copies = []
    for k in range(1, place.size(group)):
        index, device = place.peer(group, k)
        copies.append(sems.copy(base + k - 1, source(k, index), target(k, index), device))
    return copies


def add(first, *others):
    total = first.astype(F32)
    for other in others:
        total = total + other.astype(F32)
    return total.astype(BF16)


class Stream:
    phases = 6

    def __init__(self, place, order, grad, held, got_c, got_1, got_2, got_z, out, send, recv, own):
        self.place, self.order, self.grad, self.held, self.out = place, order, grad, held, out
        self.got_c, self.got_1, self.got_2, self.got_z = got_c, got_1, got_2, got_z
        self.sems, self.own = Sems(send, recv), own

    def local(self):
        if self.own is None:
            return []
        return [
            pltpu.make_async_copy(
                self.grad(2 * i + self.place.at["core"]), self.held.at[i], self.own.at[i]
            )
            for i in range(self.place.size("x"))
        ]

    def copies(self, phase):
        place, at, held = self.place, self.place.at, self.held
        nx, nz = place.size("x"), place.size("z")
        base = [0, nx, 2 * nx, 3 * nx, 3 * nx + nz, 3 * nx + 2 * nz][phase]
        sems = self.sems
        if phase == 0:
            other, device = place.peer("core", 1)
            return [
                sems.copy(i, self.grad(2 * i + other), self.got_c.at[i], device) for i in range(nx)
            ]
        if phase == 1 and self.order == "xy":
            return exchange(
                place, "x", lambda k, j: held.at[j], lambda k, j: self.got_1.at[k - 1], sems, base
            )
        if phase == 2 and self.order == "xy":
            return exchange(
                place, "y", lambda k, j: held.at[at["x"], j], lambda k, j: self.got_2.at[0], sems, base
            )
        if phase == 1:
            other, device = place.peer("y", 1)
            return [
                sems.copy(base + i, held.at[i, other], self.got_1.at[i], device) for i in range(nx)
            ]
        if phase == 2:
            return exchange(
                place,
                "x",
                lambda k, j: held.at[j, at["y"]],
                lambda k, j: self.got_2.at[k - 1],
                sems,
                base,
            )
        if phase == 3:
            return exchange(
                place,
                "z",
                lambda k, j: held.at[at["x"], at["y"], j],
                lambda k, j: self.got_z.at[k - 1],
                sems,
                base,
            )
        if phase == 4:
            piece = self.out.at[at["y"], at["z"]]
            return exchange(place, "z", lambda k, j: piece, lambda k, j: piece, sems, base)
        half = self.out.at[at["y"]]
        return exchange(place, "y", lambda k, j: half, lambda k, j: half, sems, base)

    def start(self, phase):
        for copy in self.copies(phase) + (self.local() if phase == 0 else []):
            copy.start()

    def finish(self, phase):
        for copy in self.copies(phase) + (self.local() if phase == 0 else []):
            copy.wait()
        at, held = self.place.at, self.held
        nx, nz = self.place.size("x"), self.place.size("z")
        if phase == 0:
            for i in range(nx):
                for y in range(2):
                    own = held[i, y] if self.own is not None else self.grad(2 * i + at["core"])[y]
                    held[i, y] = add(own, self.got_c[i, y])
        elif phase == 1 and self.order == "xy":
            for y in range(2):
                held[at["x"], y] = add(
                    held[at["x"], y], *[self.got_1[k, y] for k in range(nx - 1)]
                )
        elif phase == 1:
            for i in range(nx):
                held[i, at["y"]] = add(held[i, at["y"]], self.got_1[i])
        elif phase == 2:
            count = 1 if self.order == "xy" else nx - 1
            held[at["x"], at["y"]] = add(
                held[at["x"], at["y"]], *[self.got_2[k] for k in range(count)]
            )
        elif phase == 3:
            self.out[at["y"], at["z"]] = add(
                held[at["x"], at["y"], at["z"]], *[self.got_z[k] for k in range(nz - 1)]
            )


def stream_scratch(sizes, order, rows, lanes):
    nx, nz = sizes["x"], sizes["z"]
    count = 3 * nx + 2 * nz + 1
    piece = (nz, rows, lanes)
    first = (nx - 1, 2) if order == "xy" else (nx,)
    second = (1,) if order == "xy" else (nx - 1,)
    return [
        pltpu.VMEM((nx, 2) + piece, BF16),
        pltpu.VMEM((nx, 2) + piece, BF16),
        pltpu.VMEM(first + piece, BF16),
        pltpu.VMEM(second + piece, BF16),
        pltpu.VMEM((nz - 1,) + piece[1:], BF16),
        pltpu.VMEM((2,) + piece, BF16),
        pltpu.SemaphoreType.DMA((count,)),
        pltpu.SemaphoreType.DMA((count,)),
        pltpu.SemaphoreType.DMA((nx,)),
    ]


class Small:
    def __init__(self, place, combine, slots, send, recv):
        self.place, self.combine, self.slots, self.sems = place, combine, slots, Sems(send, recv)

    def offsets(self, phase):
        sizes = [self.place.size(g) for g in GROUPS]
        return sum(sizes[:phase]), sum(sizes[:phase]) - phase

    def copies(self, phase):
        slot, sem = self.offsets(phase)
        return exchange(
            self.place,
            GROUPS[phase],
            lambda k, j: self.slots.at[slot],
            lambda k, j: self.slots.at[slot + k],
            self.sems,
            sem,
        )

    def start(self, phase, values):
        self.slots[self.offsets(phase)[0]] = values
        for copy in self.copies(phase):
            copy.start()

    def finish(self, phase):
        for copy in self.copies(phase):
            copy.wait()
        slot = self.offsets(phase)[0]
        count, me = self.place.size(GROUPS[phase]), self.place.at[GROUPS[phase]]
        total = None
        for member in range(count):
            term = self.slots[slot + (me + count - member) % count]
            total = term if total is None else self.combine(total, term)
        return total


def small_scratch(sizes, rows, lanes):
    total = sum(sizes[g] for g in GROUPS)
    return [
        pltpu.VMEM((total, rows, lanes), F32),
        pltpu.SemaphoreType.DMA((total - 4,)),
        pltpu.SemaphoreType.DMA((total - 4,)),
    ]


class Gather:
    def __init__(self, place, own, every, send, recv, keep):
        self.place, self.own, self.every, self.sems, self.keep = place, own, every, Sems(send, recv), keep

    def far(self):
        place = self.place
        mine = self.every.at[place.part]
        return exchange(place, "x", lambda k, j: self.own, lambda k, j: mine, self.sems, 0)

    def near(self, step):
        place = self.place
        nx = place.size("x")
        device = place.peer("core", 1)[1]
        if step == 0:
            return self.sems.copy(nx - 1, self.own, self.every.at[place.part], device)
        chip = (place.at["x"] + nx - step) % nx
        block = self.every.at[chip * 2 + place.at["core"]]
        return self.sems.copy(nx - 1 + step, block, block, device)

    def mine(self):
        return pltpu.make_async_copy(self.own, self.every.at[self.place.part], self.keep.at[0])

    def start(self):
        for copy in self.far():
            copy.start()
        self.near(0).start()
        self.mine().start()

    def forward(self):
        for copy in self.far():
            copy.wait()
        for k in range(1, self.place.size("x")):
            self.near(k).start()

    def finish(self):
        for k in range(self.place.size("x")):
            self.near(k).wait()
        self.mine().wait()


def gather_scratch(sizes):
    count = 2 * sizes["x"] - 1
    return [
        pltpu.SemaphoreType.DMA((count,)),
        pltpu.SemaphoreType.DMA((count,)),
        pltpu.SemaphoreType.DMA((1,)),
    ]


def split_rows(rows, pieces):
    return -(-rows // (pieces * 8)) * 8


def spread(values, shape):
    count = 1
    for size in shape[:-1]:
        count *= size
    if count > values.shape[0]:
        zeros = jnp.zeros((count - values.shape[0], values.shape[1]), values.dtype)
        values = jnp.concatenate([values, zeros], axis=0)
    return values.reshape(shape)


def tile_rows(rows, height, lanes):
    filled = [r if r.shape[1] == lanes else jnp.concatenate([r, jnp.zeros((1, lanes - r.shape[1]), F32)], axis=1) for r in rows]
    at = lax.broadcasted_iota(jnp.int32, (height, lanes), 0)
    total = jnp.zeros((height, lanes), F32)
    for n, r in enumerate(filled):
        total = jnp.where(at == n, r, total)
    return total


def top(values):
    peak = jnp.max(jnp.abs(values.astype(F32)), axis=0, keepdims=True)
    return jnp.max(peak, axis=1, keepdims=True)


def attend_kernel(
    sizes,
    lens,
    tok_ref,
    seg_ref,
    qkv_sh,
    qvb_sh,
    proj_sh,
    up_sh,
    down_sh,
    ub_sh,
    ints_ref,
    qkv_ref,
    probs_ref,
    ctx_ref,
    w_ref,
    step_ref,
    bias_ref,
    proj_all,
    up_all,
    down_all,
    mask_s,
    raw_all,
    bias_all,
    bias_own,
    proj_own,
    up_own,
    down_own,
    *sems,
):
    row = pl.program_id(0)
    last = pl.num_programs(0) - 1
    place = Place(sizes)
    parts = 2 * sizes["x"]
    width = D // parts
    early = [
        Gather(place, own, every, *sems[3 * n : 3 * n + 3])
        for n, (own, every) in enumerate(((qkv_sh, raw_all), (bias_own, bias_all)))
    ]
    late = [
        Gather(place, own, every, *sems[6 + 3 * n : 9 + 3 * n])
        for n, (own, every) in enumerate(
            ((up_own, up_all), (down_own, down_all), (proj_own, proj_all))
        )
    ]
    peaks = Small(place, jnp.maximum, *sems[15:18])

    @pl.when(row == 0)
    def _():
        place.greet()
        bias_own[...] = tile_rows(
            [ub_sh[...].astype(F32), qvb_sh[0:1].astype(F32), qvb_sh[1:2].astype(F32)],
            8,
            ub_sh.shape[1],
        )
        for gather in early:
            gather.start()
        tops = [top(tok_ref[...])] + [top(qkv_sh[i]) for i in range(3)]
        tops += [top(proj_sh[...]), top(up_sh[...]), top(down_sh[...])]
        total = tile_rows([jnp.broadcast_to(t, (1, LANES)) for t in tops], 8, LANES)
        for phase in range(4):
            peaks.start(phase, total)
            total = peaks.finish(phase)
        step_ref[...] = total / LEVELS
        up_own[...] = rounded(up_sh[...].astype(F32) / step_ref[5:6, 0:1]).astype(BF16)
        down_own[...] = rounded(down_sh[...].astype(F32) / step_ref[6:7, 0:1]).astype(BF16)
        proj_own[...] = rounded(proj_sh[...].astype(F32) / step_ref[4:5, 0:1]).astype(BF16)
        for gather in early:
            gather.forward()
        for gather in late:
            gather.start()
        for gather in early:
            gather.finish()
        bias_ref[...] = bias_all[...]
        for t in range(parts):
            for i in range(3):
                w_ref[i, :, t * width : (t + 1) * width] = rounded(
                    raw_all[t, i].astype(F32) / step_ref[1 + i : 2 + i, 0:1]
                ).astype(BF16)

    @pl.when(row == last)
    def _():
        for gather in late:
            gather.forward()

    step_tokens = step_ref[0:1, 0:1]
    tok = tok_ref[pl.ds(pl.multiple_of(row * SEQ, SEQ), SEQ), :]
    ints = rounded(tok.astype(F32) / step_tokens).astype(BF16)
    ints_ref[...] = ints
    biases = [
        jnp.concatenate([bias_all[t, r : r + 1, :width] for t in range(parts)], axis=1)
        for r in (1, 2)
    ]
    for i in range(3):
        raw = dot_nn(ints, w_ref[i]) * (step_tokens * step_ref[1 + i : 2 + i, 0:1])
        if i == 0:
            raw = (raw + biases[0]) * SCORE_SCALE
        if i == 2:
            raw = raw + biases[1]
        qkv_ref[:, i * D : (i + 1) * D] = raw.astype(BF16)
    seg_q = seg_ref[0].astype(F32)
    length = lens[row]
    spot = lax.broadcasted_iota(jnp.int32, (8, SEQ), 1)
    seg_k = jnp.where(spot < length, jnp.broadcast_to(seg_q, (8, SEQ)), -1.0)
    seg_k = jnp.transpose(seg_k)[:, 0:1]
    for n, (k0, k1, q0, q1) in enumerate(TILES):
        keys = lax.broadcasted_iota(jnp.int32, (k1 - k0, q1 - q0), 0) + k0
        queries = lax.broadcasted_iota(jnp.int32, (k1 - k0, q1 - q0), 1) + q0
        allowed = (seg_k[k0:k1] == seg_q[:, q0:q1]) | (keys == queries)
        mask_s[n] = jnp.where(allowed, 0.0, MASKED)

    def pair_step(p, carry):
        at = pl.multiple_of(p * LANES, LANES)
        q_pair = qkv_ref[:, pl.ds(at, LANES)]
        k_pair = qkv_ref[:, pl.ds(D + at, LANES)]
        v_pair = qkv_ref[:, pl.ds(2 * D + at, LANES)]
        v_t = jnp.transpose(v_pair)
        parts = []
        for h in range(2):
            q_head = jnp.where(head_mask(h, SEQ), q_pair, jnp.zeros_like(q_pair))
            scores = [
                dot_nt(k_pair[k0:k1], q_head[q0:q1]) + mask_s[n]
                for n, (k0, k1, q0, q1) in enumerate(TILES)
            ]
            peak = [jnp.max(s, axis=0, keepdims=True) for s in scores]
            high = jnp.concatenate(
                [
                    peak[0][:, :128],
                    jnp.maximum(peak[0][:, 128:], peak[1][:, :256]),
                    peak[1][:, 256:],
                ],
                axis=1,
            )
            weights = [
                jnp.exp2(s - high[:, q0:q1]) for s, (k0, k1, q0, q1) in zip(scores, TILES)
            ]
            totals = both(*[jnp.sum(w, axis=0, keepdims=True) for w in weights])
            inverse = 1.0 / totals
            outs = []
            for n, (k0, k1, q0, q1) in enumerate(TILES):
                probs = (weights[n] * inverse[:, q0:q1]).astype(BF16)
                probs_ref[0, 2 * p + h, n] = probs
                outs.append(dot_nn(v_t[h * 64 : h * 64 + 64, k0:k1], probs))
            parts.append(both(*outs))
        context_t = jnp.concatenate(parts, axis=0)
        ctx_ref[:, pl.ds(at, LANES)] = jnp.transpose(context_t).astype(BF16)
        return carry

    lax.fori_loop(0, PAIRS, pair_step, 0)

    @pl.when(row == last)
    def _():
        for gather in late:
            gather.finish()


def attend(sizes, lens, tokens, segments, qkv_w, qv_bias, proj_w, up_w, down_w, up_b):
    rows = tokens.shape[0] // SEQ
    parts = 2 * sizes["x"]
    hbm = pl.BlockSpec(memory_space=pl.ANY)
    gathered = [(w.shape, BF16) for w in (proj_w, up_w, down_w)]

    def whole(*shape):
        return pl.BlockSpec(shape, lambda i, *_: (0,) * len(shape))

    return pl.pallas_call(
        lambda *refs: attend_kernel(sizes, *refs),
        name="attend",
        grid_spec=pltpu.PrefetchScalarGridSpec(
            num_scalar_prefetch=1,
            grid=(rows,),
            in_specs=[
                whole(*tokens.shape),
                pl.BlockSpec((1, 1, SEQ), lambda i, *_: (i, 0, 0)),
                whole(*qkv_w.shape),
                whole(*qv_bias.shape),
                whole(*proj_w.shape),
                whole(*up_w.shape),
                whole(*down_w.shape),
                whole(*up_b.shape),
            ],
            out_specs=[
                pl.BlockSpec((SEQ, D), lambda i, *_: (i, 0)),
                pl.BlockSpec((SEQ, 3 * D), lambda i, *_: (i, 0)),
                pl.BlockSpec((1, HEADS, 2, 256, 384), lambda i, *_: (i, 0, 0, 0, 0)),
                pl.BlockSpec((SEQ, D), lambda i, *_: (i, 0)),
                whole(3, D, D),
                whole(8, LANES),
                whole(parts, 8, up_b.shape[1]),
                hbm,
                hbm,
                hbm,
            ],
            scratch_shapes=[
                pltpu.VMEM((2, 256, 384), F32),
                pltpu.VMEM((parts,) + qkv_w.shape, BF16),
                pltpu.VMEM((parts, 8, up_b.shape[1]), F32),
                pltpu.VMEM((8, up_b.shape[1]), F32),
            ]
            + [pltpu.VMEM(w.shape, BF16) for w in (proj_w, up_w, down_w)]
            + sum([gather_scratch(sizes) for _ in range(5)], [])
            + small_scratch(sizes, 8, LANES),
        ),
        out_shape=[
            jax.ShapeDtypeStruct((rows * SEQ, D), BF16),
            jax.ShapeDtypeStruct((rows * SEQ, 3 * D), BF16),
            jax.ShapeDtypeStruct((rows, HEADS, 2, 256, 384), BF16),
            jax.ShapeDtypeStruct((rows * SEQ, D), BF16),
            jax.ShapeDtypeStruct((3, D, D), BF16),
            jax.ShapeDtypeStruct((8, LANES), F32),
            jax.ShapeDtypeStruct((parts, 8, up_b.shape[1]), F32),
        ]
        + [jax.ShapeDtypeStruct((parts,) + w.shape, BF16) for w in (proj_w, up_w, down_w)],
        compiler_params=pltpu.CompilerParams(
            vmem_limit_bytes=VMEM_LIMIT, collective_id=0, has_side_effects=True
        ),
        cost_estimate=pl.CostEstimate(
            flops=rows * 3 * 10**9, bytes_accessed=rows * 6 * 10**6, transcendentals=rows * 2 * 10**6
        ),
    )(lens, tokens, segments, qkv_w, qv_bias, proj_w, up_w, down_w, up_b)

GELU_P = 0.3275911 * 0.7071067811865476
GELU_A = (0.254829592, -0.284496736, 1.421413741, -1.453152027, 1.061405429)
INV_SQRT_2PI = 0.3989422804014327


def gelu_pair(pre):
    base = 1.0 + GELU_P * jnp.abs(pre)
    t = pl.reciprocal(base, approx=True)
    t = t * (2.0 - base * t)
    bell = jnp.exp2(pre * pre * (-0.5 * LOG2E))
    poly = 0.5 * GELU_A[4]
    for a in (GELU_A[3], GELU_A[2], GELU_A[1], GELU_A[0]):
        poly = poly * t + 0.5 * a
    tail = poly * t * bell
    cdf = jnp.where(pre < 0.0, tail, 1.0 - tail)
    return pre * cdf, cdf + (pre * INV_SQRT_2PI) * bell


def fold_rows(values):
    total = values[0:8]
    for r in range(8, values.shape[0], 8):
        total = total + values[r : r + 8]
    return total


def normalize(values):
    centred = values - jnp.mean(values, axis=-1, keepdims=True)
    inverse = lax.rsqrt(jnp.mean(centred * centred, axis=-1, keepdims=True) + EPS)
    return centred * inverse, inverse


def norm_back(scaled, standard, inverse):
    return inverse * (
        scaled
        - jnp.mean(scaled, axis=-1, keepdims=True)
        - standard * jnp.mean(scaled * standard, axis=-1, keepdims=True)
    )


TB = 256


def ffn_kernel(
    step_ref,
    bias_ref,
    tok_ref,
    ctx_ref,
    og_ref,
    proj_ref,
    up_ref,
    down_ref,
    pb_ref,
    fg_ref,
    fs_ref,
    db_ref,
    sg_ref,
    ss_ref,
    out_ref,
    first_ref,
    gctx_ref,
    dproj_ref,
    dup_ref,
    ddown_ref,
    dub_ref,
    dvec_ref,
    act_s,
    slope_s,
    dproj_s,
    dup_s,
    ddown_s,
    dub_s,
    dvec_s,
):
    at = pl.program_id(0)
    last = pl.num_programs(0) - 1
    parts = up_ref.shape[0]
    step_proj, step_up, step_down = [step_ref[r : r + 1, 0:1] for r in (4, 5, 6)]

    @pl.when(at == 0)
    def _():
        dproj_s[...] = jnp.zeros_like(dproj_s)
        dup_s[...] = jnp.zeros_like(dup_s)
        ddown_s[...] = jnp.zeros_like(ddown_s)
        dub_s[...] = jnp.zeros_like(dub_s)
        dvec_s[...] = jnp.zeros_like(dvec_s)

    proj_bias, first_gain, first_shift, down_bias, second_gain, second_shift = [
        r[...].astype(F32) for r in (pb_ref, fg_ref, fs_ref, db_ref, sg_ref, ss_ref)
    ]
    ctx = ctx_ref[...]
    first_in = tok_ref[...].astype(F32) + (dot_nn(ctx, proj_ref[...]) * step_proj + proj_bias)
    n1, r1 = normalize(first_in)
    normed = n1 * first_gain + first_shift
    low = normed.astype(BF16)
    branch = None
    for t in range(parts):
        pre = dot_nn(low, up_ref[t]) * step_up + bias_ref[t, 0:1]
        act, slope = gelu_pair(pre)
        act = act.astype(BF16)
        act_s[t] = act
        slope_s[t] = slope
        term = dot_nn(act, down_ref[t])
        branch = term if branch is None else branch + term
    second_in = normed + (branch * step_down + down_bias)
    n2, r2 = normalize(second_in)
    out_ref[...] = (n2 * second_gain + second_shift).astype(BF16)
    og = og_ref[...].astype(F32)
    grad_second = norm_back(og * second_gain, n2, r2)
    dvec_s[4] += fold_rows(og * n2)
    dvec_s[5] += fold_rows(og)
    dvec_s[3] += fold_rows(grad_second)
    grad_down = (grad_second * step_down).astype(BF16)
    back = grad_second
    for t in range(parts):
        grad_pre = dot_nt(grad_down, down_ref[t]) * slope_s[t]
        dub_s[t] += fold_rows(grad_pre)
        grad_up = (grad_pre * step_up).astype(BF16)
        back = back + dot_nt(grad_up, up_ref[t])
        dup_s[t] += dot_tn(low, grad_up)
        ddown_s[t] += dot_tn(grad_down, act_s[t])
    dvec_s[1] += fold_rows(back * n1)
    dvec_s[2] += fold_rows(back)
    grad_first = norm_back(back * first_gain, n1, r1)
    dvec_s[0] += fold_rows(grad_first)
    first_ref[...] = grad_first
    grad_proj = (grad_first * step_proj).astype(BF16)
    dproj_s[...] += dot_tn(ctx, grad_proj)
    gctx_ref[...] = dot_nt(grad_proj, proj_ref[...]).astype(BF16)

    @pl.when(at == last)
    def _():
        width = D // parts
        for t in range(parts):
            rows = dproj_s[t * width : (t + 1) * width]
            dproj_ref[t] = spread(rows.astype(BF16), dproj_ref.shape[1:])
            dup_ref[t] = spread(dup_s[t].astype(BF16), dup_ref.shape[1:])
            ddown_ref[t] = spread(ddown_s[t].astype(BF16), ddown_ref.shape[1:])
            dub_ref[t] = jnp.sum(dub_s[t], axis=0, keepdims=True)
        dvec_ref[...] = jnp.sum(dvec_s[...], axis=1)


def feed_forward(sizes, steps, biases, tokens, ctx, out_grad, proj, up, down, vecs):
    count = tokens.shape[0]
    parts, nz = 2 * sizes["x"], sizes["z"]
    wide = FF // parts
    split = (parts, 2, 2, nz, split_rows(D, 4 * nz), wide)
    split_proj = (parts, 2, nz, split_rows(D // parts, 2 * nz), D)
    block = pl.BlockSpec((TB, D), lambda i, *_: (i, 0))

    def whole(*shape):
        return pl.BlockSpec(shape, lambda i, *_: (0,) * len(shape))

    return pl.pallas_call(
        ffn_kernel,
        name="feed_forward",
        grid=(count // TB,),
        in_specs=[
            whole(8, LANES),
            whole(parts, 8, wide),
            block,
            block,
            block,
            whole(D, D),
            whole(parts, D, wide),
            whole(parts, wide, D),
        ]
        + [whole(1, D)] * 6,
        out_specs=[
            block,
            block,
            block,
            whole(*split_proj),
            whole(*split),
            whole(*split),
            whole(parts, 1, wide),
            whole(6, D),
        ],
        scratch_shapes=[
            pltpu.VMEM((parts, TB, wide), BF16),
            pltpu.VMEM((parts, TB, wide), F32),
            pltpu.VMEM((D, D), F32),
            pltpu.VMEM((parts, D, wide), F32),
            pltpu.VMEM((parts, D, wide), F32),
            pltpu.VMEM((parts, 8, wide), F32),
            pltpu.VMEM((6, 8, D), F32),
        ],
        out_shape=[
            jax.ShapeDtypeStruct((count, D), BF16),
            jax.ShapeDtypeStruct((count, D), F32),
            jax.ShapeDtypeStruct((count, D), BF16),
            jax.ShapeDtypeStruct(split_proj, BF16),
            jax.ShapeDtypeStruct(split, BF16),
            jax.ShapeDtypeStruct(split, BF16),
            jax.ShapeDtypeStruct((parts, 1, wide), F32),
            jax.ShapeDtypeStruct((6, D), F32),
        ],
        compiler_params=pltpu.CompilerParams(vmem_limit_bytes=VMEM_LIMIT),
        cost_estimate=pl.CostEstimate(
            flops=count * 14 * 10**6, bytes_accessed=count * 12000, transcendentals=count * 4096
        ),
    )(steps, biases, tokens, ctx, out_grad, proj, up, down, *[v.reshape(1, D) for v in vecs])


PLANS = (
    ((0, 2), (2, 5), (5, 7), (7, 9), (9, 12), (12, 14)),
    ((0, 2), (2, 5), (5, 7), (7, 10), (10, 12), (12, 14)),
    ((0, 2), (4, 7), (7, 9), (9, 11), (11, 14), (14, 16)),
    ((0, 2), (4, 7), (7, 9), (9, 12), (12, 14), (14, 16)),
    ((0, 2), (6, 8), (8, 10), (10, 12), (12, 14), (14, 16)),
)
ORDERS = ("xy", "yx", "xy", "yx", "xy", "xy", "yx")


def passing(grads, weights, step):
    return jnp.where(weights.astype(F32) == 0.0, 0.0, grads.astype(F32)) / step


def back_kernel(
    sizes,
    step_ref,
    tok_ref,
    ints_ref,
    qkv_ref,
    probs_ref,
    ctx_ref,
    gctx_ref,
    first_ref,
    w_ref,
    dproj_hbm,
    dup_hbm,
    ddown_hbm,
    dub_ref,
    dvec_ref,
    qkv_sh,
    proj_sh,
    up_sh,
    down_sh,
    tg_ref,
    dqkv_out,
    dqv_out,
    dproj_out,
    dup_out,
    dub_out,
    ddown_out,
    vec_out,
    grad_s,
    dqkv_s,
    dqv_s,
    part_s,
    *scratch,
):
    step = pl.program_id(0)
    rows = grad_s.shape[0]
    place = Place(sizes)
    parts = 2 * sizes["x"]
    width = D // parts
    step_tokens = step_ref[0:1, 0:1]
    sources = [
        lambda t: dup_hbm.at[t, 0],
        lambda t: ddown_hbm.at[t, 0],
        lambda t: dup_hbm.at[t, 1],
        lambda t: ddown_hbm.at[t, 1],
        lambda t: dproj_hbm.at[t],
        lambda t: part_s.at[t, 0],
        lambda t: part_s.at[t, 1],
    ]
    streams = []
    for n, source in enumerate(sources):
        refs = scratch[9 * n : 9 * n + 9]
        own = refs[8] if n < 5 else None
        streams.append(Stream(place, ORDERS[n], source, *refs[:8], own))
    sums = Small(place, jnp.add, *scratch[63:66])

    @pl.when(step == 0)
    def _():
        dqkv_s[...] = jnp.zeros_like(dqkv_s)
        dqv_s[...] = jnp.zeros_like(dqv_s)
        place.greet()

    def advance(tick):
        for now in range(16):
            done = [(s, k) for s, plan in enumerate(PLANS) for k, p in enumerate(plan) if p[1] == now]
            begun = [(s, k) for s, plan in enumerate(PLANS) for k, p in enumerate(plan) if p[0] == now]
            if done or begun:

                @pl.when(tick == now)
                def _():
                    for s, k in done:
                        streams[s].finish(k)
                    for s, k in begun:
                        streams[s].start(k)

    def pair_step(p, carry):
        for n in range(16 // (PAIRS * rows)):
            advance((step * PAIRS + p) * (16 // (PAIRS * rows)) + n)
        at = pl.multiple_of(p * LANES, LANES)
        q_pair = qkv_ref[:, pl.ds(at, LANES)]
        k_pair = qkv_ref[:, pl.ds(D + at, LANES)]
        v_pair = qkv_ref[:, pl.ds(2 * D + at, LANES)]
        g_pair = gctx_ref[:, pl.ds(at, LANES)]
        c_pair = ctx_ref[:, pl.ds(at, LANES)]
        k_t = jnp.transpose(k_pair)
        product = (g_pair.astype(F32) * c_pair.astype(F32)).astype(BF16)
        d_keys = [None, None]
        d_values = [None, None]
        parts = []
        for h in range(2):
            mask = head_mask(h, SEQ)
            q_head = jnp.where(mask, q_pair, jnp.zeros_like(q_pair))
            g_head = jnp.where(mask, g_pair, jnp.zeros_like(g_pair))
            ones = jnp.where(head_mask(h, 8), 1.0, 0.0).astype(BF16)
            centre = dot_nt(ones, product)[0:1]
            outs = []
            for n, (k0, k1, q0, q1) in enumerate(TILES):
                probs = probs_ref[0, 2 * p + h, n]
                gp = dot_nt(v_pair[k0:k1], g_head[q0:q1])
                gs = (probs.astype(F32) * (gp - centre[:, q0:q1])).astype(BF16)
                dv = dot_nn(probs, g_head[q0:q1])
                dk = dot_nn(gs, q_head[q0:q1])
                d_values[n] = dv if h == 0 else d_values[n] + dv
                d_keys[n] = dk if h == 0 else d_keys[n] + dk
                outs.append(dot_nn(k_t[h * 64 : h * 64 + 64, k0:k1], gs))
            parts.append(both(*outs))
        d_q = jnp.transpose(jnp.concatenate(parts, axis=0)) * 0.125
        dqv_s[0, :, pl.ds(at, LANES)] += fold_rows(d_q)
        grad_s[step, :, pl.ds(at, LANES)] = (d_q * (step_tokens * step_ref[1:2, 0:1])).astype(BF16)
        for n, (k0, k1, q0, q1) in enumerate(TILES):
            grad_s[step, k0:k1, pl.ds(D + at, LANES)] = (
                d_keys[n] * (step_tokens * step_ref[2:3, 0:1] * (1.0 / LOG2E))
            ).astype(BF16)
            dqv_s[1, :, pl.ds(at, LANES)] += fold_rows(d_values[n])
            grad_s[step, k0:k1, pl.ds(2 * D + at, LANES)] = (
                d_values[n] * (step_tokens * step_ref[3:4, 0:1])
            ).astype(BF16)
        return carry

    @pl.when(step < rows)
    def _():
        lax.fori_loop(0, PAIRS, pair_step, 0)
        for i in range(3):
            dqkv_s[i] += dot_tn(grad_s[step, :, i * D : (i + 1) * D], ints_ref[...])

    @pl.when(step == rows)
    def _():
        for t in range(parts):
            piece = jnp.concatenate(
                [dqkv_s[i, t * width : (t + 1) * width] for i in range(3)], axis=0
            )
            part_s[t] = spread(piece.astype(BF16), part_s.shape[1:])
        for stream in streams[5:]:
            stream.start(0)
        dqv = jnp.sum(dqv_s[...], axis=1)
        vec = [dvec_ref[r : r + 1] for r in range(6)] + [dqv[0:1], dqv[1:2]]
        dub = jnp.concatenate([dub_ref[t] for t in range(parts)], axis=1)
        vec += [dub[:, r * D : (r + 1) * D] for r in range(4)]
        sums.start(0, tile_rows(vec, 16, D))
        for s, plan in enumerate(PLANS):
            for k, p in enumerate(plan):
                if p[1] == 16:
                    streams[s].finish(k)

    def settle(tick):
        for stream in streams[5:]:
            stream.finish(tick)
        if tick < 5:
            for stream in streams[5:]:
                stream.start(tick + 1)
        if tick < 3:
            sums.start(tick + 1, sums.finish(tick))
        if tick == 3:
            total = sums.finish(tick)
            for n, r in enumerate((0, 1, 2, 3, 4, 5)):
                vec_out[n] = total[r : r + 1]
            for t in range(parts):

                @pl.when(place.part == t)
                def _():
                    dqv_out[...] = total[6:8, t * width : (t + 1) * width]
                    wide = FF // parts
                    dub_out[...] = total[
                        8 + t * wide // D : 9 + t * wide // D, t * wide % D : t * wide % D + wide
                    ]

    @pl.when(step == rows + 1)
    def _():
        settle(0)

    @pl.when(step >= rows)
    def _():
        grads = grad_s[step - rows]
        total = None
        for i in range(3):
            term = dot_nt(grads[:, i * D : (i + 1) * D], w_ref[i])
            total = term if total is None else total + term
        tg_ref[...] = first_ref[...] + passing(total, tok_ref[...], step_tokens)

    @pl.when(step == 2 * rows - 1)
    def _():
        settle(1)
        halves = [
            jnp.concatenate([streams[n + h].out[...].reshape(D // 2, FF // parts) for h in (0, 2)], axis=0)
            for n in range(2)
        ]
        dup_out[...] = passing(halves[0], up_sh[...], step_ref[5:6, 0:1])
        ddown_out[...] = passing(
            jnp.transpose(halves[1].astype(F32)), down_sh[...], step_ref[6:7, 0:1]
        )
        settle(2)
        settle(3)
        settle(4)
        dproj = streams[4].out[...].reshape(-1, D)[:width]
        dproj_out[...] = passing(dproj, proj_sh[...], step_ref[4:5, 0:1])
        settle(5)
        whole = jnp.concatenate(
            [streams[5 + h].out[...].reshape(-1, D) for h in range(2)], axis=0
        ).astype(F32)
        for i in range(3):
            dqkv_out[i] = passing(
                jnp.transpose(whole[i * width : (i + 1) * width]),
                qkv_sh[i],
                step_ref[1 + i : 2 + i, 0:1],
            )


def attend_back(
    sizes, steps, tokens, ints, qkv, probs, ctx, gctx, first, qkv_full, dproj, dup, ddown, dub, dvec,
    qkv_w, proj_w, up_w, down_w,
):
    rows = tokens.shape[0] // SEQ
    parts, nz = 2 * sizes["x"], sizes["z"]
    width, wide = D // parts, FF // parts
    part = (parts, 2, 2, nz, split_rows(3 * width, 4 * nz), D)
    pieces = [dup.shape[-2:], ddown.shape[-2:], dup.shape[-2:], ddown.shape[-2:], dproj.shape[-2:]]
    pieces += [part[-2:]] * 2
    early = lambda i: (jnp.minimum(i, rows - 1), 0)
    late = lambda i: (jnp.maximum(i - rows, 0), 0)
    hbm = pl.BlockSpec(memory_space=pl.ANY)

    def whole(*shape):
        return pl.BlockSpec(shape, lambda i: (0,) * len(shape))

    outs = [
        ((3, D, width), F32),
        ((2, width), F32),
        ((width, D), F32),
        ((D, wide), F32),
        ((1, wide), F32),
        ((wide, D), F32),
        ((6, 1, D), F32),
    ]
    return pl.pallas_call(
        lambda *refs: back_kernel(sizes, *refs),
        name="attend_back",
        grid=(2 * rows,),
        in_specs=[
            whole(8, LANES),
            pl.BlockSpec((SEQ, D), late),
            pl.BlockSpec((SEQ, D), early),
            pl.BlockSpec((SEQ, 3 * D), early),
            pl.BlockSpec(
                (1, HEADS, 2, 256, 384), lambda i: (jnp.minimum(i, rows - 1), 0, 0, 0, 0)
            ),
            pl.BlockSpec((SEQ, D), early),
            pl.BlockSpec((SEQ, D), early),
            pl.BlockSpec((SEQ, D), late),
            whole(3, D, D),
            hbm,
            hbm,
            hbm,
            whole(*dub.shape),
            whole(*dvec.shape),
            whole(*qkv_w.shape),
            whole(*proj_w.shape),
            whole(*up_w.shape),
            whole(*down_w.shape),
        ],
        out_specs=[pl.BlockSpec((SEQ, D), late)] + [whole(*shape) for shape, _ in outs],
        scratch_shapes=[
            pltpu.VMEM((rows, SEQ, 3 * D), BF16),
            pltpu.VMEM((3, D, D), F32),
            pltpu.VMEM((2, 8, D), F32),
            pltpu.VMEM(part, BF16),
        ]
        + sum([stream_scratch(sizes, o, *p) for o, p in zip(ORDERS, pieces)], [])
        + small_scratch(sizes, 16, D),
        out_shape=[jax.ShapeDtypeStruct((rows * SEQ, D), F32)]
        + [jax.ShapeDtypeStruct(shape, kind) for shape, kind in outs],
        compiler_params=pltpu.CompilerParams(
            vmem_limit_bytes=VMEM_LIMIT, collective_id=1, has_side_effects=True
        ),
        cost_estimate=pl.CostEstimate(
            flops=rows * 6 * 10**9, bytes_accessed=rows * 8 * 10**6, transcendentals=0
        ),
    )(
        steps, tokens, ints, qkv, probs, ctx, gctx, first, qkv_full, dproj, dup, ddown, dub, dvec,
        qkv_w, proj_w, up_w, down_w,
    )

def local(
    tokens,
    segment_ids,
    row_lengths,
    qkv_weight,
    qv_bias,
    proj_weight,
    proj_bias,
    first_gain,
    first_shift,
    up_weight,
    up_bias,
    down_weight,
    down_bias,
    second_gain,
    second_shift,
    out_grad,
):
    rows = tokens.shape[0] // SEQ
    place = lax.axis_index("tensor")
    sizes = group_sizes(lax.axis_size("tensor"), lax.axis_size("dp"))
    segments = lax.dynamic_slice(segment_ids, (place * rows, 0), (rows, SEQ))
    lengths = lax.dynamic_slice(row_lengths, (place * rows,), (rows,))
    ints, qkv, probs, ctx, qkv_full, steps, biases, proj_full, up_full, down_full = attend(
        sizes,
        lengths,
        tokens,
        segments[:, None, :],
        qkv_weight,
        qv_bias,
        proj_weight,
        up_weight,
        down_weight,
        up_bias[None],
    )
    vecs = (proj_bias, first_gain, first_shift, down_bias, second_gain, second_shift)
    layer_out, grad_first, grad_ctx, dproj, dup, ddown, dub, dvec = feed_forward(
        sizes, steps, biases, tokens, ctx, out_grad, proj_full.reshape(D, D), up_full, down_full, vecs
    )
    tokens_grad, dqkv, dqv, dproj, dup, dub, ddown, vec = attend_back(
        sizes, steps, tokens, ints, qkv, probs, ctx, grad_ctx, grad_first, qkv_full,
        dproj, dup, ddown, dub, dvec, qkv_weight, proj_weight, up_weight, down_weight,
    )
    vec = [vec[n, 0] for n in range(6)]
    return (
        layer_out, tokens_grad, dqkv, dqv, dproj, vec[0], vec[1], vec[2], dup, dub[0], ddown,
        vec[3], vec[4], vec[5],
    )


def solution(mesh):
    in_specs = (
        P(("dp", "tensor"), None),
        P("dp", None),
        P("dp"),
        P(None, None, "tensor"),
        P(None, "tensor"),
        P("tensor", None),
        P(),
        P(),
        P(),
        P(None, "tensor"),
        P("tensor"),
        P("tensor", None),
        P(),
        P(),
        P(),
        P(("dp", "tensor"), None),
    )
    out_specs = (
        P(("dp", "tensor"), None),
        P(("dp", "tensor"), None),
        P(None, None, "tensor"),
        P(None, "tensor"),
        P("tensor", None),
        P(),
        P(),
        P(),
        P(None, "tensor"),
        P("tensor"),
        P("tensor", None),
        P(),
        P(),
        P(),
    )
    return jax.shard_map(local, mesh=mesh, in_specs=in_specs, out_specs=out_specs, check_vma=False)
```

time: 1000 us -> 234 us (0.23)
  matrix products: 409 us -> 0 us
  waiting for transfers between devices: 227 us -> 0 us
  Pallas kernels: 0 us -> 216 us
  blocking collectives: 124 us -> 0 us
  local copies, waits for them, and re-layouts: 131 us -> 17.4 us
  other arithmetic: 84.1 us -> 0 us
  between operations: 18.7 us -> 0.74 us
    dot_general x68 -> x0, matrix products: 409 us -> none  [the longest x8 64.8 us: attend_back(): jnp.einsum('rhqk,rkhe->rqhe', grad_scores, keys_low, preferred_element_ty...]
    pallas_call x0 -> x3, Pallas kernels: none -> 216 us  [the longest x1 96.1 us: attend_back(): pl.pallas_call(lambda *refs: back_kernel(sizes, *refs), name='attend_back...]
    reduce_scatter x4 -> x0, waiting for transfers between devices: 125 us -> none  [the longest x2 125 us: reduce_rows(): lax.psum_scatter(term_fn(jnp.int32(0), lax.axis_size('tensor') * own_rows...]
    all_gather x4 -> x0, waiting for transfers between devices: 101 us -> none  [the longest x2 80.2 us: group_rows(): return lax.all_gather(values, 'tensor', axis=0, tiled=True)]
    psum x2 -> x0, blocking collectives: 63 us -> none  [the longest x1 40.8 us: local(): lax.psum((proj_bias_grad, first_gain_grad, first_shift_grad, down_bias_gr...]
    pmax x2 -> x0, blocking collectives: 49.2 us -> none  [the longest x1 42.2 us: local(): peak_tokens = lax.pmax(jnp.max(jnp.abs(token_vals)), ('dp', 'tensor'))]
    while x4 -> x0, local copies, waits for them, and re-layouts: 29.6 us -> none  [the longest x3 25.4 us: local(): lax.map(attend_back, (queries, keys_low, values_low, pair_segments, pair_...]
    reduce_sum x16 -> x0, other arithmetic: 27.7 us -> none  [the longest x8 7.79 us: attend_pair(): totals = jnp.sum(weights, axis=-1, keepdims=True)]
  transfers between devices with their start and end apart: 9 -> 0, of which waited for: 6 -> 0; matrix products, arithmetic and copies ran while one was open for 44% -> 0% of each run, Pallas kernels for 0% -> 0%
where the time goes in v1:
time: 234 us
  Pallas kernels  216 us (92%)
  local copies, waits for them, and re-layouts  17.4 us (7%)
    pallas_call x1, Pallas kernels, attend_back(): pl.pallas_call(lambda *refs: back_kernel(sizes, *refs), name='attend_back...  96.1 us
    pallas_call x1, Pallas kernels, feed_forward(): pl.pallas_call(ffn_kernel, name='feed_forward', grid=(count // TB,), in_s...  60.3 us
    pallas_call x1, Pallas kernels, attend(): pl.pallas_call(lambda *refs: attend_kernel(sizes, *refs), name='attend',...  59.1 us
    unnamed x33, local copies, waits for them, and re-layouts  9.45 us

profile of v1, /device:TPU:0, one launch (start us, length us, event | category | flops | bytes accessed | tf_op | source)
XLA Modules:
  0.0 233.6 jit_solution(14127733723184290965)
XLA Ops:
  0.6 0.0 copy-start
  0.7 1.2 dynamic_slice.6.refs_0_
  1.9 0.0 copy-done
  1.9 0.6 broadcast_in_dim.6.refs_2_
  2.5 1.3 broadcast_in_dim.7.refs_8_
  3.8 0.0 copy-start.6
  3.8 0.0 copy-start.7
  3.8 0.0 copy-start.8
  3.8 0.0 copy-start.9
  3.8 0.0 copy-start.10
  3.8 0.0 copy-start.11
  3.8 59.1 %attend.1 = (bf16[2048,512]{1,0:T(8,128)(2,1)}, bf16[2048,1536]{1,0:T(8,128)(2,1)}, bf16[4,8,2,256,384]{4,3,2,1,0:T(8,128)(2,1)}, bf16[2048,512]{1,0:T(8,128)(2,...) custom-call(s32[4]{0:T(128)} %dynamic_slice.6.refs_0_, ...), custom_call_target="tpu_custom_call" | custom-call | flops 12000000000 | bytes 24000000 | tf_op jit(solution)/shard_map/attend/pallas_call | solution.py:523
  63.0 0.0 copy-done.6
  63.0 0.6 reshape.50.pb_ref
  63.6 0.0 copy-done.7
  63.6 0.6 reshape.51.fg_ref
  64.1 0.0 copy-done.8
  64.1 0.6 reshape.52.fs_ref
  64.7 0.0 copy-done.9
  64.7 0.6 reshape.53.db_ref
  65.3 0.0 copy-done.10
  65.3 0.6 reshape.54.sg_ref
  65.9 0.0 copy-done.11
  65.9 0.6 reshape.55.ss_ref
  66.5 60.3 %feed_forward.1 = (bf16[2048,512]{1,0:T(8,128)(2,1)}, f32[2048,512]{1,0:T(8,128)}, bf16[2048,512]{1,0:T(8,128)(2,1)}, bf16[4,2,4,16,512]{4,3,2,1,0:T(8,128)(2,1)...) custom-call(f32[8,128]{1,0:T(8,128)} %get-tuple-element.40.step_ref., ...), custom_call_target="tpu_custom_call" | custom-call | flops 28672000000 | bytes 24576000 | tf_op jit(solution)/shard_map/feed_forward/pallas_call | solution.py:731
  126.8 96.1 %attend_back.1 = (f32[2048,512]{1,0:T(8,128)}, f32[3,512,128]{2,1,0:T(8,128)}, f32[2,128]{1,0:T(2,128)}, f32[128,512]{1,0:T(8,128)}, f32[512,512]{1,0:T(8,128)},...) custom-call(f32[8,128]{1,0:T(8,128)} %get-tuple-element.40.step_ref.refs_0_, ...), custom_call_target="tpu_custom_call" | custom-call | flops 24000000000 | bytes 32000000 | tf_op jit(solution)/shard_map/attend_back/pallas_call | solution.py:1029
  222.9 1.3 fusion
  224.2 0.0 copy-start.3
  224.2 0.0 copy-start.12
  224.2 0.0 copy-start.4
  224.2 4.7 %copy.37 = f32[2048,512]{1,0:T(8,128)} copy(f32[2048,512]{1,0:T(8,128)} %get-tuple-element.87) | data formatting | bytes 8388608
  228.9 0.0 copy-done.3
  228.9 0.0 copy-start.2
  228.9 0.0 copy-start.5
  229.0 0.0 copy-start.1
  229.0 0.9 copy.38
  229.8 0.0 copy-done.12
  229.8 0.6 copy.39
  230.4 0.0 copy-done.4
  230.4 0.7 copy.40
  231.1 0.0 copy-done.2
  231.1 1.0 copy.41
  232.1 0.0 copy-done.5
  232.1 0.6 copy.42
  232.7 0.0 copy-done.1
  232.7 1.0 copy.43
  (1 shorter events, 0.0 us)
Async XLA Ops:
  0.6 1.3 copy-start
  3.8 59.2 %copy-start.6 = (bf16[512]{0:T(512)(128)(2,1)S(1)}, bf16[512]{0:T(512)(128)(2,1)}, u32[]{:S(2)}) copy-start(bf16[512]{0:T(512)(128)(2,1)} %param.22) | copy-start | bytes 3076
  3.8 59.8 %copy-start.7 = (bf16[512]{0:T(512)(128)(2,1)S(1)}, bf16[512]{0:T(512)(128)(2,1)}, u32[]{:S(2)}) copy-start(bf16[512]{0:T(512)(128)(2,1)} %param.23) | copy-start | bytes 3076
  3.8 60.4 %copy-start.8 = (bf16[512]{0:T(512)(128)(2,1)S(1)}, bf16[512]{0:T(512)(128)(2,1)}, u32[]{:S(2)}) copy-start(bf16[512]{0:T(512)(128)(2,1)} %param.24) | copy-start | bytes 3076
  3.8 60.9 %copy-start.9 = (bf16[512]{0:T(512)(128)(2,1)S(1)}, bf16[512]{0:T(512)(128)(2,1)}, u32[]{:S(2)}) copy-start(bf16[512]{0:T(512)(128)(2,1)} %param.28) | copy-start | bytes 3076
  3.8 61.5 %copy-start.10 = (bf16[512]{0:T(512)(128)(2,1)S(1)}, bf16[512]{0:T(512)(128)(2,1)}, u32[]{:S(2)}) copy-start(bf16[512]{0:T(512)(128)(2,1)} %param.29) | copy-start | bytes 3076
  3.8 62.1 %copy-start.11 = (bf16[512]{0:T(512)(128)(2,1)S(1)}, bf16[512]{0:T(512)(128)(2,1)}, u32[]{:S(2)}) copy-start(bf16[512]{0:T(512)(128)(2,1)} %param.30) | copy-start | bytes 3076
  224.2 4.7 %copy-start.3 = (f32[3,512,128]{2,1,0:T(8,128)S(1)}, f32[3,512,128]{2,1,0:T(8,128)}, u32[]{:S(2)}) copy-start(f32[3,512,128]{2,1,0:T(8,128)} %get-tuple-element.88) | copy-start | bytes 2359300
  224.2 5.6 %copy-start.12 = (f32[2,128]{1,0:T(2,128)S(1)}, f32[2,128]{1,0:T(2,128)}, u32[]{:S(2)}) copy-start(f32[2,128]{1,0:T(2,128)} %get-tuple-element.89) | copy-start | bytes 3076
  224.2 6.2 %copy-start.4 = (f32[128,512]{1,0:T(8,128)S(1)}, f32[128,512]{1,0:T(8,128)}, u32[]{:S(2)}) copy-start(f32[128,512]{1,0:T(8,128)} %get-tuple-element.90) | copy-start | bytes 786436
  228.9 2.2 copy-start.2
  228.9 3.1 %copy-start.5 = (f32[1,512]{1,0:T(1,128)S(1)}, f32[1,512]{1,0:T(1,128)}, u32[]{:S(2)}) copy-start(f32[1,512]{1,0:T(1,128)} %get-tuple-element.64) | copy-start | bytes 6148
  229.0 3.7 %copy-start.1 = (f32[512,512]{1,0:T(8,128)S(1)}, f32[512,512]{1,0:T(8,128)}, u32[]{:S(2)}) copy-start(f32[512,512]{1,0:T(8,128)} %get-tuple-element.96) | copy-start | bytes 3145732

commit v2 on v1

--- a/solution.py
+++ b/solution.py
@@ -52,11 +52,18 @@
 
 
 MESH = pl.DeviceIdType.MESH
-GROUPS = ("core", "x", "y", "z")
+MESH_AXES = ("tensor", "dp")
 
 
 def group_sizes(tensor_size, dp_size):
-    return {"core": 2, "x": tensor_size // 2, "y": 2, "z": dp_size // 2}
+    return {
+        "core": 2,
+        "x": tensor_size // 2,
+        "y": 2,
+        "z": dp_size // 2,
+        "tensor": tensor_size,
+        "dp": dp_size,
+    }
 
 
 class Place:
@@ -64,12 +71,16 @@
         t, d = lax.axis_index("tensor"), lax.axis_index("dp")
         self.sizes = sizes
         self.part = t
-        self.at = {"core": t % 2, "x": t // 2, "y": d % 2, "z": d // 2}
+        self.at = {"core": t % 2, "x": t // 2, "y": d % 2, "z": d // 2, "tensor": t, "dp": d}
 
     def size(self, group):
         return self.sizes[group]
 
     def peer(self, group, k):
+        if group in MESH_AXES:
+            at = {axis: lax.axis_index(axis) for axis in MESH_AXES}
+            at[group] = (at[group] + k) % self.sizes[group]
+            return at[group], (at["dp"], at["tensor"])
         at = dict(self.at)
         at[group] = (at[group] + k) % self.sizes[group]
         return at[group], (at["z"] * 2 + at["y"], at["x"] * 2 + at["core"])
@@ -77,7 +88,7 @@
     def greet(self):
         barrier = pltpu.get_barrier_semaphore()
         count = 0
-        for group in GROUPS:
+        for group in MESH_AXES:
             for k in range(1, self.sizes[group]):
                 pl.semaphore_signal(
                     barrier, inc=1, device_id=self.peer(group, k)[1], device_id_type=MESH
@@ -238,14 +249,14 @@
         self.place, self.combine, self.slots, self.sems = place, combine, slots, Sems(send, recv)
 
     def offsets(self, phase):
-        sizes = [self.place.size(g) for g in GROUPS]
+        sizes = [self.place.size(g) for g in MESH_AXES]
         return sum(sizes[:phase]), sum(sizes[:phase]) - phase
 
     def copies(self, phase):
         slot, sem = self.offsets(phase)
         return exchange(
             self.place,
-            GROUPS[phase],
+            MESH_AXES[phase],
             lambda k, j: self.slots.at[slot],
             lambda k, j: self.slots.at[slot + k],
             self.sems,
@@ -261,7 +272,7 @@
         for copy in self.copies(phase):
             copy.wait()
         slot = self.offsets(phase)[0]
-        count, me = self.place.size(GROUPS[phase]), self.place.at[GROUPS[phase]]
+        count, me = self.place.size(MESH_AXES[phase]), self.place.at[MESH_AXES[phase]]
         total = None
         for member in range(count):
             term = self.slots[slot + (me + count - member) % count]
@@ -270,11 +281,11 @@
 
 
 def small_scratch(sizes, rows, lanes):
-    total = sum(sizes[g] for g in GROUPS)
+    total = sum(sizes[g] for g in MESH_AXES)
     return [
         pltpu.VMEM((total, rows, lanes), F32),
-        pltpu.SemaphoreType.DMA((total - 4,)),
-        pltpu.SemaphoreType.DMA((total - 4,)),
+        pltpu.SemaphoreType.DMA((total - 2,)),
+        pltpu.SemaphoreType.DMA((total - 2,)),
     ]
 
 
@@ -357,7 +368,7 @@
 
 def attend_kernel(
     sizes,
-    lens,
+    len_ref,
     tok_ref,
     seg_ref,
     qkv_sh,
@@ -406,16 +417,16 @@
     def _():
         place.greet()
         bias_own[...] = tile_rows(
-            [ub_sh[...].astype(F32), qvb_sh[0:1].astype(F32), qvb_sh[1:2].astype(F32)],
+            [ub_sh[...].astype(F32)[None], qvb_sh[0:1].astype(F32), qvb_sh[1:2].astype(F32)],
             8,
-            ub_sh.shape[1],
+            ub_sh.shape[0],
         )
         for gather in early:
             gather.start()
         tops = [top(tok_ref[...])] + [top(qkv_sh[i]) for i in range(3)]
         tops += [top(proj_sh[...]), top(up_sh[...]), top(down_sh[...])]
         total = tile_rows([jnp.broadcast_to(t, (1, LANES)) for t in tops], 8, LANES)
-        for phase in range(4):
+        for phase in range(2):
             peaks.start(phase, total)
             total = peaks.finish(phase)
         step_ref[...] = total / LEVELS
@@ -455,8 +466,9 @@
         if i == 2:
             raw = raw + biases[1]
         qkv_ref[:, i * D : (i + 1) * D] = raw.astype(BF16)
-    seg_q = seg_ref[0].astype(F32)
-    length = lens[row]
+    here = place.part * pl.num_programs(0) + row
+    seg_q = seg_ref[pl.ds(here, 1), :].astype(F32)
+    length = len_ref[here]
     spot = lax.broadcasted_iota(jnp.int32, (8, SEQ), 1)
     seg_k = jnp.where(spot < length, jnp.broadcast_to(seg_q, (8, SEQ)), -1.0)
     seg_k = jnp.transpose(seg_k)[:, 0:1]
@@ -524,11 +536,12 @@
         lambda *refs: attend_kernel(sizes, *refs),
         name="attend",
         grid_spec=pltpu.PrefetchScalarGridSpec(
-            num_scalar_prefetch=1,
+            num_scalar_prefetch=0,
             grid=(rows,),
             in_specs=[
+                pl.BlockSpec(memory_space=pltpu.SMEM),
                 whole(*tokens.shape),
-                pl.BlockSpec((1, 1, SEQ), lambda i, *_: (i, 0, 0)),
+                whole(*segments.shape),
                 whole(*qkv_w.shape),
                 whole(*qv_bias.shape),
                 whole(*proj_w.shape),
@@ -543,7 +556,7 @@
                 pl.BlockSpec((SEQ, D), lambda i, *_: (i, 0)),
                 whole(3, D, D),
                 whole(8, LANES),
-                whole(parts, 8, up_b.shape[1]),
+                whole(parts, 8, up_b.shape[0]),
                 hbm,
                 hbm,
                 hbm,
@@ -551,8 +564,8 @@
             scratch_shapes=[
                 pltpu.VMEM((2, 256, 384), F32),
                 pltpu.VMEM((parts,) + qkv_w.shape, BF16),
-                pltpu.VMEM((parts, 8, up_b.shape[1]), F32),
-                pltpu.VMEM((8, up_b.shape[1]), F32),
+                pltpu.VMEM((parts, 8, up_b.shape[0]), F32),
+                pltpu.VMEM((8, up_b.shape[0]), F32),
             ]
             + [pltpu.VMEM(w.shape, BF16) for w in (proj_w, up_w, down_w)]
             + sum([gather_scratch(sizes) for _ in range(5)], [])
@@ -565,7 +578,7 @@
             jax.ShapeDtypeStruct((rows * SEQ, D), BF16),
             jax.ShapeDtypeStruct((3, D, D), BF16),
             jax.ShapeDtypeStruct((8, LANES), F32),
-            jax.ShapeDtypeStruct((parts, 8, up_b.shape[1]), F32),
+            jax.ShapeDtypeStruct((parts, 8, up_b.shape[0]), F32),
         ]
         + [jax.ShapeDtypeStruct((parts,) + w.shape, BF16) for w in (proj_w, up_w, down_w)],
         compiler_params=pltpu.CompilerParams(
@@ -576,21 +589,12 @@
         ),
     )(lens, tokens, segments, qkv_w, qv_bias, proj_w, up_w, down_w, up_b)
 
-GELU_P = 0.3275911 * 0.7071067811865476
-GELU_A = (0.254829592, -0.284496736, 1.421413741, -1.453152027, 1.061405429)
 INV_SQRT_2PI = 0.3989422804014327
 
 
 def gelu_pair(pre):
-    base = 1.0 + GELU_P * jnp.abs(pre)
-    t = pl.reciprocal(base, approx=True)
-    t = t * (2.0 - base * t)
+    cdf = 0.5 + 0.5 * lax.erf(pre * 0.7071067811865476)
     bell = jnp.exp2(pre * pre * (-0.5 * LOG2E))
-    poly = 0.5 * GELU_A[4]
-    for a in (GELU_A[3], GELU_A[2], GELU_A[1], GELU_A[0]):
-        poly = poly * t + 0.5 * a
-    tail = poly * t * bell
-    cdf = jnp.where(pre < 0.0, tail, 1.0 - tail)
     return pre * cdf, cdf + (pre * INV_SQRT_2PI) * bell
 
 
@@ -615,7 +619,7 @@
     )
 
 
-TB = 256
+TB = 512
 
 
 def ffn_kernel(
@@ -663,7 +667,7 @@
         dvec_s[...] = jnp.zeros_like(dvec_s)
 
     proj_bias, first_gain, first_shift, down_bias, second_gain, second_shift = [
-        r[...].astype(F32) for r in (pb_ref, fg_ref, fs_ref, db_ref, sg_ref, ss_ref)
+        r[...].astype(F32)[None] for r in (pb_ref, fg_ref, fs_ref, db_ref, sg_ref, ss_ref)
     ]
     ctx = ctx_ref[...]
     first_in = tok_ref[...].astype(F32) + (dot_nn(ctx, proj_ref[...]) * step_proj + proj_bias)
@@ -671,9 +675,11 @@
     normed = n1 * first_gain + first_shift
     low = normed.astype(BF16)
     branch = None
+    pre = dot_nn(low, up_ref[0])
     for t in range(parts):
-        pre = dot_nn(low, up_ref[t]) * step_up + bias_ref[t, 0:1]
-        act, slope = gelu_pair(pre)
+        follow = dot_nn(low, up_ref[t + 1]) if t + 1 < parts else None
+        act, slope = gelu_pair(pre * step_up + bias_ref[t, 0:1])
+        pre = follow
         act = act.astype(BF16)
         act_s[t] = act
         slope_s[t] = slope
@@ -689,8 +695,11 @@
     dvec_s[3] += fold_rows(grad_second)
     grad_down = (grad_second * step_down).astype(BF16)
     back = grad_second
+    grad_act = dot_nt(grad_down, down_ref[0])
     for t in range(parts):
-        grad_pre = dot_nt(grad_down, down_ref[t]) * slope_s[t]
+        follow = dot_nt(grad_down, down_ref[t + 1]) if t + 1 < parts else None
+        grad_pre = grad_act * slope_s[t]
+        grad_act = follow
         dub_s[t] += fold_rows(grad_pre)
         grad_up = (grad_pre * step_up).astype(BF16)
         back = back + dot_nt(grad_up, up_ref[t])
@@ -742,7 +751,7 @@
             whole(parts, D, wide),
             whole(parts, wide, D),
         ]
-        + [whole(1, D)] * 6,
+        + [whole(D)] * 6,
         out_specs=[
             block,
             block,
@@ -776,17 +785,21 @@
         cost_estimate=pl.CostEstimate(
             flops=count * 14 * 10**6, bytes_accessed=count * 12000, transcendentals=count * 4096
         ),
-    )(steps, biases, tokens, ctx, out_grad, proj, up, down, *[v.reshape(1, D) for v in vecs])
+    )(steps, biases, tokens, ctx, out_grad, proj, up, down, *vecs)
 
 
 PLANS = (
-    ((0, 2), (2, 5), (5, 7), (7, 9), (9, 12), (12, 14)),
-    ((0, 2), (2, 5), (5, 7), (7, 10), (10, 12), (12, 14)),
-    ((0, 2), (4, 7), (7, 9), (9, 11), (11, 14), (14, 16)),
-    ((0, 2), (4, 7), (7, 9), (9, 12), (12, 14), (14, 16)),
-    ((0, 2), (6, 8), (8, 10), (10, 12), (12, 14), (14, 16)),
+    ((0, 2), (2, 6), (6, 9), (9, 11), (11, 13), (13, 16)),
+    ((0, 2), (4, 8), (8, 11), (12, 14), (14, 16), (16, 20)),
+    ((0, 2), (7, 11), (11, 14), (15, 18), (18, 21), (21, 27)),
+    ((0, 3), (9, 13), (14, 17), (17, 20), (20, 24), (24, 31)),
+    ((0, 3), (12, 15), (15, 18), (18, 22), (22, 26), (28, 35)),
+    ((16, 19), (19, 23), (23, 29), (29, 32), (32, 36), (36, 39)),
+    ((16, 19), (19, 23), (23, 28), (28, 30), (30, 34), (34, 38)),
+    ((16, 19), (19, 25), (25, 33), (33, 37), (37, 40), (40, 41)),
 )
-ORDERS = ("xy", "yx", "xy", "yx", "xy", "xy", "yx")
+ORDERS = ('xy', 'xy', 'xy', 'xy', 'xy', 'xy', 'yx', 'xy')
+THIRDS = 3
 
 
 def passing(grads, weights, step):
@@ -839,15 +852,14 @@
         lambda t: dup_hbm.at[t, 1],
         lambda t: ddown_hbm.at[t, 1],
         lambda t: dproj_hbm.at[t],
-        lambda t: part_s.at[t, 0],
-        lambda t: part_s.at[t, 1],
     ]
+    sources += [lambda t, q=q: part_s.at[t, q] for q in range(THIRDS)]
     streams = []
     for n, source in enumerate(sources):
         refs = scratch[9 * n : 9 * n + 9]
         own = refs[8] if n < 5 else None
         streams.append(Stream(place, ORDERS[n], source, *refs[:8], own))
-    sums = Small(place, jnp.add, *scratch[63:66])
+    sums = Small(place, jnp.add, *scratch[9 * len(sources) :])
 
     @pl.when(step == 0)
     def _():
@@ -855,22 +867,24 @@
         dqv_s[...] = jnp.zeros_like(dqv_s)
         place.greet()
 
-    def advance(tick):
-        for now in range(16):
-            done = [(s, k) for s, plan in enumerate(PLANS) for k, p in enumerate(plan) if p[1] == now]
-            begun = [(s, k) for s, plan in enumerate(PLANS) for k, p in enumerate(plan) if p[0] == now]
-            if done or begun:
-
-                @pl.when(tick == now)
-                def _():
-                    for s, k in done:
-                        streams[s].finish(k)
-                    for s, k in begun:
-                        streams[s].start(k)
+    def events(now):
+        for s, plan in enumerate(PLANS):
+            for k, p in enumerate(plan):
+                if p[1] == now:
+                    streams[s].finish(k)
+        for s, plan in enumerate(PLANS):
+            for k, p in enumerate(plan):
+                if p[0] == now:
+                    streams[s].start(k)
+
+    def advance(tick, ticks):
+        for now in ticks:
+            if any(now in p for plan in PLANS for p in plan):
+                pl.when(tick == now)(lambda: events(now))
 
     def pair_step(p, carry):
         for n in range(16 // (PAIRS * rows)):
-            advance((step * PAIRS + p) * (16 // (PAIRS * rows)) + n)
+            advance((step * PAIRS + p) * (16 // (PAIRS * rows)) + n, range(16))
         at = pl.multiple_of(p * LANES, LANES)
         q_pair = qkv_ref[:, pl.ds(at, LANES)]
         k_pair = qkv_ref[:, pl.ds(D + at, LANES)]
@@ -925,43 +939,34 @@
                 [dqkv_s[i, t * width : (t + 1) * width] for i in range(3)], axis=0
             )
             part_s[t] = spread(piece.astype(BF16), part_s.shape[1:])
-        for stream in streams[5:]:
-            stream.start(0)
         dqv = jnp.sum(dqv_s[...], axis=1)
         vec = [dvec_ref[r : r + 1] for r in range(6)] + [dqv[0:1], dqv[1:2]]
         dub = jnp.concatenate([dub_ref[t] for t in range(parts)], axis=1)
         vec += [dub[:, r * D : (r + 1) * D] for r in range(4)]
         sums.start(0, tile_rows(vec, 16, D))
-        for s, plan in enumerate(PLANS):
-            for k, p in enumerate(plan):
-                if p[1] == 16:
-                    streams[s].finish(k)
-
-    def settle(tick):
-        for stream in streams[5:]:
-            stream.finish(tick)
-        if tick < 5:
-            for stream in streams[5:]:
-                stream.start(tick + 1)
-        if tick < 3:
-            sums.start(tick + 1, sums.finish(tick))
-        if tick == 3:
-            total = sums.finish(tick)
-            for n, r in enumerate((0, 1, 2, 3, 4, 5)):
-                vec_out[n] = total[r : r + 1]
-            for t in range(parts):
-
-                @pl.when(place.part == t)
-                def _():
-                    dqv_out[...] = total[6:8, t * width : (t + 1) * width]
-                    wide = FF // parts
-                    dub_out[...] = total[
-                        8 + t * wide // D : 9 + t * wide // D, t * wide % D : t * wide % D + wide
-                    ]
+
+    @pl.when(step >= rows)
+    def _():
+        for n in range(4 // rows):
+            advance(16 + (step - rows) * (4 // rows) + n, range(16, 20))
+
+    def vectors():
+        total = sums.finish(1)
+        for n in range(6):
+            vec_out[n] = total[n : n + 1]
+        for t in range(parts):
+
+            @pl.when(place.part == t)
+            def _():
+                dqv_out[...] = total[6:8, t * width : (t + 1) * width]
+                wide = FF // parts
+                dub_out[...] = total[
+                    8 + t * wide // D : 9 + t * wide // D, t * wide % D : t * wide % D + wide
+                ]
 
     @pl.when(step == rows + 1)
     def _():
-        settle(0)
+        sums.start(1, sums.finish(0))
 
     @pl.when(step >= rows)
     def _():
@@ -970,27 +975,32 @@
         for i in range(3):
             term = dot_nt(grads[:, i * D : (i + 1) * D], w_ref[i])
             total = term if total is None else total + term
-        tg_ref[...] = first_ref[...] + passing(total, tok_ref[...], step_tokens)
+        tg_ref[...] = (first_ref[...] + passing(total, tok_ref[...], step_tokens)).astype(BF16)
+
+    def joined(*group):
+        halves = [streams[n].out[...].reshape(D // 2, FF // parts) for n in group]
+        return jnp.concatenate(halves, axis=0)
 
     @pl.when(step == 2 * rows - 1)
     def _():
-        settle(1)
-        halves = [
-            jnp.concatenate([streams[n + h].out[...].reshape(D // 2, FF // parts) for h in (0, 2)], axis=0)
-            for n in range(2)
-        ]
-        dup_out[...] = passing(halves[0], up_sh[...], step_ref[5:6, 0:1])
-        ddown_out[...] = passing(
-            jnp.transpose(halves[1].astype(F32)), down_sh[...], step_ref[6:7, 0:1]
-        )
-        settle(2)
-        settle(3)
-        settle(4)
-        dproj = streams[4].out[...].reshape(-1, D)[:width]
-        dproj_out[...] = passing(dproj, proj_sh[...], step_ref[4:5, 0:1])
-        settle(5)
+        ticks = sorted({n for plan in PLANS for p in plan for n in p if n >= 20})
+        ended = [max(PLANS[s][5][1] for s in group) for group in ((0, 2), (1, 3), (4,))]
+        for now in [19] + ticks:
+            if now > 19:
+                events(now)
+            if now == ticks[len(ticks) // 3]:
+                vectors()
+            if now == max(19, ended[0]):
+                dup_out[...] = passing(joined(0, 2), up_sh[...], step_ref[5:6, 0:1])
+            if now == max(19, ended[1]):
+                ddown_out[...] = passing(
+                    jnp.transpose(joined(1, 3).astype(F32)), down_sh[...], step_ref[6:7, 0:1]
+                )
+            if now == max(19, ended[2]):
+                dproj = streams[4].out[...].reshape(-1, D)[:width]
+                dproj_out[...] = passing(dproj, proj_sh[...], step_ref[4:5, 0:1])
         whole = jnp.concatenate(
-            [streams[5 + h].out[...].reshape(-1, D) for h in range(2)], axis=0
+            [streams[5 + q].out[...].reshape(-1, D) for q in range(THIRDS)], axis=0
         ).astype(F32)
         for i in range(3):
             dqkv_out[i] = passing(
@@ -1007,9 +1017,9 @@
     rows = tokens.shape[0] // SEQ
     parts, nz = 2 * sizes["x"], sizes["z"]
     width, wide = D // parts, FF // parts
-    part = (parts, 2, 2, nz, split_rows(3 * width, 4 * nz), D)
+    part = (parts, THIRDS, 2, nz, split_rows(3 * width, 2 * THIRDS * nz), D)
     pieces = [dup.shape[-2:], ddown.shape[-2:], dup.shape[-2:], ddown.shape[-2:], dproj.shape[-2:]]
-    pieces += [part[-2:]] * 2
+    pieces += [part[-2:]] * THIRDS
     early = lambda i: (jnp.minimum(i, rows - 1), 0)
     late = lambda i: (jnp.maximum(i - rows, 0), 0)
     hbm = pl.BlockSpec(memory_space=pl.ANY)
@@ -1061,7 +1071,7 @@
         ]
         + sum([stream_scratch(sizes, o, *p) for o, p in zip(ORDERS, pieces)], [])
         + small_scratch(sizes, 16, D),
-        out_shape=[jax.ShapeDtypeStruct((rows * SEQ, D), F32)]
+        out_shape=[jax.ShapeDtypeStruct((rows * SEQ, D), BF16)]
         + [jax.ShapeDtypeStruct(shape, kind) for shape, kind in outs],
         compiler_params=pltpu.CompilerParams(
             vmem_limit_bytes=VMEM_LIMIT, collective_id=1, has_side_effects=True
@@ -1093,21 +1103,18 @@
     out_grad,
 ):
     rows = tokens.shape[0] // SEQ
-    place = lax.axis_index("tensor")
     sizes = group_sizes(lax.axis_size("tensor"), lax.axis_size("dp"))
-    segments = lax.dynamic_slice(segment_ids, (place * rows, 0), (rows, SEQ))
-    lengths = lax.dynamic_slice(row_lengths, (place * rows,), (rows,))
     ints, qkv, probs, ctx, qkv_full, steps, biases, proj_full, up_full, down_full = attend(
         sizes,
-        lengths,
+        row_lengths,
         tokens,
-        segments[:, None, :],
+        segment_ids,
         qkv_weight,
         qv_bias,
         proj_weight,
         up_weight,
         down_weight,
-        up_bias[None],
+        up_bias,
     )
     vecs = (proj_bias, first_gain, first_shift, down_bias, second_gain, second_shift)
     layer_out, grad_first, grad_ctx, dproj, dup, ddown, dub, dvec = feed_forward(
@@ -1119,7 +1126,7 @@
     )
     vec = [vec[n, 0] for n in range(6)]
     return (
-        layer_out, tokens_grad, dqkv, dqv, dproj, vec[0], vec[1], vec[2], dup, dub[0], ddown,
+        layer_out, tokens_grad.astype(F32), dqkv, dqv, dproj, vec[0], vec[1], vec[2], dup, dub[0], ddown,
         vec[3], vec[4], vec[5],
     )
 

time: 234 us -> 201 us (0.86)
  Pallas kernels: 216 us -> 191 us
  local copies, waits for them, and re-layouts: 17.4 us -> 5.29 us
  other arithmetic: 0 us -> 4.28 us
    pallas_call x1, Pallas kernels: 60.3 us -> 45.1 us  [feed_forward(): pl.pallas_call(ffn_kernel, name='feed_forward', grid=(count // TB,), in_s...]
    pallas_call x1, Pallas kernels: 96.1 us -> 86.9 us  [attend_back(): pl.pallas_call(lambda *refs: back_kernel(sizes, *refs), name='attend_back...]
    unnamed x33 -> x20, local copies, waits for them, and re-layouts: 9.45 us -> 4.69 us
    convert_element_type x0 -> x1, other arithmetic: none -> 4.28 us  [local(): tokens_grad.astype(F32)]
    reshape x6 -> x0, local copies, waits for them, and re-layouts: 3.49 us -> none  [feed_forward(): v.reshape(1, D)]
where the time goes in v2:
time: 201 us
  Pallas kernels  191 us (95%)
  local copies, waits for them, and re-layouts  5.29 us (3%)
  other arithmetic  4.28 us (2%)
    pallas_call x1, Pallas kernels, attend_back(): pl.pallas_call(lambda *refs: back_kernel(sizes, *refs), name='attend_back...  86.9 us
    pallas_call x1, Pallas kernels, attend(): pl.pallas_call(lambda *refs: attend_kernel(sizes, *refs), name='attend',...  59 us
    pallas_call x1, Pallas kernels, feed_forward(): pl.pallas_call(ffn_kernel, name='feed_forward', grid=(count // TB,), in_s...  45.1 us
    unnamed x20, local copies, waits for them, and re-layouts  4.69 us
    convert_element_type x1, other arithmetic, local(): tokens_grad.astype(F32)  4.28 us

profile of v2, /device:TPU:0, one launch (start us, length us, event | category | flops | bytes accessed | tf_op | source)
XLA Modules:
  0.0 201.3 jit_solution(17318922709877514744)
XLA Ops:
  0.6 59.0 %attend.1 = (bf16[2048,512]{1,0:T(8,128)(2,1)}, bf16[2048,1536]{1,0:T(8,128)(2,1)}, bf16[4,8,2,256,384]{4,3,2,1,0:T(8,128)(2,1)}, bf16[2048,512]{1,0:T(8,128)(2,...) custom-call(s32[16]{0:T(128)} %refs_0_.1, ...), custom_call_target="tpu_custom_call" | custom-call | flops 12000000000 | bytes 24000000 | tf_op jit(solution)/shard_map/attend/pallas_call | solution.py:535
  59.7 45.1 %feed_forward.1 = (bf16[2048,512]{1,0:T(8,128)(2,1)}, f32[2048,512]{1,0:T(8,128)}, bf16[2048,512]{1,0:T(8,128)(2,1)}, bf16[4,2,4,16,512]{4,3,2,1,0:T(8,128)(2,1)...) custom-call(f32[8,128]{1,0:T(8,128)} %get-tuple-element.40.step_ref., ...), custom_call_target="tpu_custom_call" | custom-call | flops 28672000000 | bytes 24576000 | tf_op jit(solution)/shard_map/feed_forward/pallas_call | solution.py:740
  104.7 86.9 %attend_back.1 = (bf16[2048,512]{1,0:T(8,128)(2,1)}, f32[3,512,128]{2,1,0:T(8,128)}, f32[2,128]{1,0:T(2,128)}, f32[128,512]{1,0:T(8,128)}, f32[512,512]{1,0:T(8,...) custom-call(f32[8,128]{1,0:T(8,128)} %get-tuple-element.40.step_ref.refs_0_, ...), custom_call_target="tpu_custom_call" | custom-call | flops 24000000000 | bytes 32000000 | tf_op jit(solution)/shard_map/attend_back/pallas_call | solution.py:1039
  191.7 0.0 copy-start.4
  191.7 0.0 copy-start.2
  191.7 0.0 copy-start.6
  191.7 0.0 copy-start.3
  191.7 4.3 %convert_element_type.3 = f32[2048,512]{1,0:T(8,128)} convert(bf16[2048,512]{1,0:T(8,128)(2,1)} %get-tuple-element.58) | non-fusion elementwise | flops 1048576 | bytes 6291456 | tf_op jit(solution)/shard_map/convert_element_type | solution.py:1129
  196.0 0.0 copy-start.1
  196.0 0.0 copy-done.4
  196.0 0.6 fusion
  196.6 0.0 copy-done.2
  196.6 0.0 copy-start.5
  196.6 0.0 copy-start
  196.6 0.9 copy.36
  197.5 0.0 copy-done.6
  197.5 0.6 copy.37
  198.1 0.0 copy-done.3
  198.1 0.7 copy.38
  198.8 0.0 copy-done.1
  198.8 1.0 copy.39
  199.7 0.0 copy-done.5
  199.7 0.6 copy.40
  200.3 0.0 copy-done
  200.3 1.0 copy.41
Async XLA Ops:
  191.7 4.3 %copy-start.4 = (f32[6,1,512]{2,1,0:T(1,128)S(1)}, f32[6,1,512]{2,1,0:T(1,128)}, u32[]{:S(2)}) copy-start(f32[6,1,512]{2,1,0:T(1,128)} %get-tuple-element.62) | copy-start | bytes 36868
  191.7 4.9 %copy-start.2 = (f32[3,512,128]{2,1,0:T(8,128)S(1)}, f32[3,512,128]{2,1,0:T(8,128)}, u32[]{:S(2)}) copy-start(f32[3,512,128]{2,1,0:T(8,128)} %get-tuple-element.88) | copy-start | bytes 2359300
  191.7 5.8 %copy-start.6 = (f32[2,128]{1,0:T(2,128)S(1)}, f32[2,128]{1,0:T(2,128)}, u32[]{:S(2)}) copy-start(f32[2,128]{1,0:T(2,128)} %get-tuple-element.89) | copy-start | bytes 3076
  191.7 6.4 %copy-start.3 = (f32[128,512]{1,0:T(8,128)S(1)}, f32[128,512]{1,0:T(8,128)}, u32[]{:S(2)}) copy-start(f32[128,512]{1,0:T(8,128)} %get-tuple-element.90) | copy-start | bytes 786436
  196.0 2.8 %copy-start.1 = (f32[512,512]{1,0:T(8,128)S(1)}, f32[512,512]{1,0:T(8,128)}, u32[]{:S(2)}) copy-start(f32[512,512]{1,0:T(8,128)} %get-tuple-element.94) | copy-start | bytes 3145732
  196.6 3.1 %copy-start.5 = (f32[1,512]{1,0:T(1,128)S(1)}, f32[1,512]{1,0:T(1,128)}, u32[]{:S(2)}) copy-start(f32[1,512]{1,0:T(1,128)} %get-tuple-element.64) | copy-start | bytes 6148
  196.6 3.7 %copy-start = (f32[512,512]{1,0:T(8,128)S(1)}, f32[512,512]{1,0:T(8,128)}, u32[]{:S(2)}) copy-start(f32[512,512]{1,0:T(8,128)} %get-tuple-element.96) | copy-start | bytes 3145732

commit v3 on v2

--- a/solution.py
+++ b/solution.py
@@ -45,10 +45,20 @@
     return (lane < HEAD_DIM) if head == 0 else (lane >= HEAD_DIM)
 
 
+def stacked(pair):
+    zeros = jnp.zeros_like(pair)
+    return jnp.concatenate(
+        [jnp.where(head_mask(h, pair.shape[0]), pair, zeros) for h in range(2)], axis=0
+    )
+
+
+def unstacked(blocks):
+    rows = blocks.shape[0] // 2
+    return jnp.where(head_mask(0, rows), blocks[:rows], blocks[rows:])
+
+
 def both(left, right):
-    return jnp.concatenate(
-        [left[:, :128], left[:, 128:] + right[:, :256], right[:, 256:]], axis=1
-    )
+    return jnp.concatenate([left[:128], left[128:] + right[:256], right[256:]], axis=0)
 
 
 MESH = pl.DeviceIdType.MESH
@@ -415,28 +425,27 @@
 
     @pl.when(row == 0)
     def _():
-        place.greet()
         bias_own[...] = tile_rows(
             [ub_sh[...].astype(F32)[None], qvb_sh[0:1].astype(F32), qvb_sh[1:2].astype(F32)],
             8,
             ub_sh.shape[0],
         )
-        for gather in early:
-            gather.start()
         tops = [top(tok_ref[...])] + [top(qkv_sh[i]) for i in range(3)]
         tops += [top(proj_sh[...]), top(up_sh[...]), top(down_sh[...])]
         total = tile_rows([jnp.broadcast_to(t, (1, LANES)) for t in tops], 8, LANES)
-        for phase in range(2):
-            peaks.start(phase, total)
-            total = peaks.finish(phase)
-        step_ref[...] = total / LEVELS
+        place.greet()
+        peaks.start(0, total)
+        for gather in early:
+            gather.start()
+        peaks.start(1, peaks.finish(0))
+        step_ref[...] = peaks.finish(1) / LEVELS
+        proj_own[...] = rounded(proj_sh[...].astype(F32) / step_ref[4:5, 0:1]).astype(BF16)
         up_own[...] = rounded(up_sh[...].astype(F32) / step_ref[5:6, 0:1]).astype(BF16)
         down_own[...] = rounded(down_sh[...].astype(F32) / step_ref[6:7, 0:1]).astype(BF16)
-        proj_own[...] = rounded(proj_sh[...].astype(F32) / step_ref[4:5, 0:1]).astype(BF16)
+        for gather in late:
+            gather.start()
         for gather in early:
             gather.forward()
-        for gather in late:
-            gather.start()
         for gather in early:
             gather.finish()
         bias_ref[...] = bias_all[...]
@@ -483,36 +492,36 @@
         q_pair = qkv_ref[:, pl.ds(at, LANES)]
         k_pair = qkv_ref[:, pl.ds(D + at, LANES)]
         v_pair = qkv_ref[:, pl.ds(2 * D + at, LANES)]
-        v_t = jnp.transpose(v_pair)
-        parts = []
-        for h in range(2):
-            q_head = jnp.where(head_mask(h, SEQ), q_pair, jnp.zeros_like(q_pair))
-            scores = [
-                dot_nt(k_pair[k0:k1], q_head[q0:q1]) + mask_s[n]
-                for n, (k0, k1, q0, q1) in enumerate(TILES)
-            ]
-            peak = [jnp.max(s, axis=0, keepdims=True) for s in scores]
-            high = jnp.concatenate(
-                [
-                    peak[0][:, :128],
-                    jnp.maximum(peak[0][:, 128:], peak[1][:, :256]),
-                    peak[1][:, 256:],
-                ],
-                axis=1,
-            )
-            weights = [
-                jnp.exp2(s - high[:, q0:q1]) for s, (k0, k1, q0, q1) in zip(scores, TILES)
-            ]
-            totals = both(*[jnp.sum(w, axis=0, keepdims=True) for w in weights])
-            inverse = 1.0 / totals
-            outs = []
-            for n, (k0, k1, q0, q1) in enumerate(TILES):
-                probs = (weights[n] * inverse[:, q0:q1]).astype(BF16)
-                probs_ref[0, 2 * p + h, n] = probs
-                outs.append(dot_nn(v_t[h * 64 : h * 64 + 64, k0:k1], probs))
-            parts.append(both(*outs))
-        context_t = jnp.concatenate(parts, axis=0)
-        ctx_ref[:, pl.ds(at, LANES)] = jnp.transpose(context_t).astype(BF16)
+        scores = []
+        for n, (k0, k1, q0, q1) in enumerate(TILES):
+            s = dot_nt(stacked(k_pair[k0:k1]), q_pair[q0:q1])
+            scores.append(s.reshape(2, 256, 384) + mask_s[n])
+        peak = [jnp.max(s, axis=1, keepdims=True) for s in scores]
+        high = jnp.concatenate(
+            [
+                peak[0][:, :, :128],
+                jnp.maximum(peak[0][:, :, 128:], peak[1][:, :, :256]),
+                peak[1][:, :, 256:],
+            ],
+            axis=2,
+        )
+        weights = [jnp.exp2(s - high[:, :, q0:q1]) for s, (k0, k1, q0, q1) in zip(scores, TILES)]
+        sums = [jnp.sum(w, axis=1, keepdims=True) for w in weights]
+        totals = jnp.concatenate(
+            [
+                sums[0][:, :, :128],
+                sums[0][:, :, 128:] + sums[1][:, :, :256],
+                sums[1][:, :, 256:],
+            ],
+            axis=2,
+        )
+        inverse = 1.0 / totals
+        outs = []
+        for n, (k0, k1, q0, q1) in enumerate(TILES):
+            probs = (weights[n] * inverse[:, :, q0:q1]).astype(BF16)
+            probs_ref[0, pl.ds(2 * p, 2), n] = probs
+            outs.append(dot_tn(probs.reshape(512, 384), stacked(v_pair[k0:k1])))
+        ctx_ref[:, pl.ds(at, LANES)] = both(*outs).astype(BF16)
         return carry
 
     lax.fori_loop(0, PAIRS, pair_step, 0)
@@ -789,16 +798,16 @@
 
 
 PLANS = (
-    ((0, 2), (2, 6), (6, 9), (9, 11), (11, 13), (13, 16)),
-    ((0, 2), (4, 8), (8, 11), (12, 14), (14, 16), (16, 20)),
-    ((0, 2), (7, 11), (11, 14), (15, 18), (18, 21), (21, 27)),
-    ((0, 3), (9, 13), (14, 17), (17, 20), (20, 24), (24, 31)),
-    ((0, 3), (12, 15), (15, 18), (18, 22), (22, 26), (28, 35)),
-    ((16, 19), (19, 23), (23, 29), (29, 32), (32, 36), (36, 39)),
-    ((16, 19), (19, 23), (23, 28), (28, 30), (30, 34), (34, 38)),
-    ((16, 19), (19, 25), (25, 33), (33, 37), (37, 40), (40, 41)),
+    ((0, 2), (2, 6), (7, 10), (10, 13), (13, 16), (16, 20)),
+    ((0, 2), (2, 6), (7, 10), (11, 14), (15, 19), (19, 22)),
+    ((0, 3), (4, 8), (8, 11), (12, 15), (16, 20), (21, 27)),
+    ((0, 3), (4, 8), (8, 11), (17, 21), (21, 25), (25, 33)),
+    ((0, 3), (9, 12), (12, 14), (19, 23), (23, 26), (29, 35)),
+    ((16, 19), (19, 22), (23, 29), (29, 32), (32, 37), (37, 40)),
+    ((16, 19), (19, 24), (24, 28), (28, 31), (31, 36), (36, 39)),
+    ((16, 19), (19, 24), (24, 30), (30, 34), (34, 38), (38, 41)),
 )
-ORDERS = ('xy', 'xy', 'xy', 'xy', 'xy', 'xy', 'yx', 'xy')
+ORDERS = ('xy', 'yx', 'xy', 'yx', 'xy', 'xy', 'yx', 'xy')
 THIRDS = 3
 
 
@@ -822,10 +831,6 @@
     ddown_hbm,
     dub_ref,
     dvec_ref,
-    qkv_sh,
-    proj_sh,
-    up_sh,
-    down_sh,
     tg_ref,
     dqkv_out,
     dqv_out,
@@ -891,39 +896,35 @@
         v_pair = qkv_ref[:, pl.ds(2 * D + at, LANES)]
         g_pair = gctx_ref[:, pl.ds(at, LANES)]
         c_pair = ctx_ref[:, pl.ds(at, LANES)]
-        k_t = jnp.transpose(k_pair)
         product = (g_pair.astype(F32) * c_pair.astype(F32)).astype(BF16)
-        d_keys = [None, None]
-        d_values = [None, None]
-        parts = []
-        for h in range(2):
-            mask = head_mask(h, SEQ)
-            q_head = jnp.where(mask, q_pair, jnp.zeros_like(q_pair))
-            g_head = jnp.where(mask, g_pair, jnp.zeros_like(g_pair))
-            ones = jnp.where(head_mask(h, 8), 1.0, 0.0).astype(BF16)
-            centre = dot_nt(ones, product)[0:1]
-            outs = []
-            for n, (k0, k1, q0, q1) in enumerate(TILES):
-                probs = probs_ref[0, 2 * p + h, n]
-                gp = dot_nt(v_pair[k0:k1], g_head[q0:q1])
-                gs = (probs.astype(F32) * (gp - centre[:, q0:q1])).astype(BF16)
-                dv = dot_nn(probs, g_head[q0:q1])
-                dk = dot_nn(gs, q_head[q0:q1])
-                d_values[n] = dv if h == 0 else d_values[n] + dv
-                d_keys[n] = dk if h == 0 else d_keys[n] + dk
-                outs.append(dot_nn(k_t[h * 64 : h * 64 + 64, k0:k1], gs))
-            parts.append(both(*outs))
-        d_q = jnp.transpose(jnp.concatenate(parts, axis=0)) * 0.125
+        lane = lax.broadcasted_iota(jnp.int32, (8, LANES), 1)
+        line = lax.broadcasted_iota(jnp.int32, (8, LANES), 0)
+        ones = jnp.where(lane // HEAD_DIM == line, 1.0, 0.0).astype(BF16)
+        centre = dot_nt(ones, product)
+        outs = []
+        for n, (k0, k1, q0, q1) in enumerate(TILES):
+            probs = probs_ref[0, pl.ds(2 * p, 2), n]
+            gp = dot_nt(stacked(v_pair[k0:k1]), g_pair[q0:q1])
+            gs = jnp.concatenate(
+                [
+                    (probs[h].astype(F32) * (gp[256 * h : 256 * h + 256] - centre[h : h + 1, q0:q1])).astype(BF16)
+                    for h in range(2)
+                ],
+                axis=0,
+            )
+            d_values = unstacked(dot_nn(probs.reshape(512, 384), g_pair[q0:q1]))
+            d_keys = unstacked(dot_nn(gs, q_pair[q0:q1]))
+            outs.append(dot_tn(gs, stacked(k_pair[k0:k1])))
+            grad_s[step, k0:k1, pl.ds(D + at, LANES)] = (
+                d_keys * (step_tokens * step_ref[2:3, 0:1] * (1.0 / LOG2E))
+            ).astype(BF16)
+            dqv_s[1, :, pl.ds(at, LANES)] += fold_rows(d_values)
+            grad_s[step, k0:k1, pl.ds(2 * D + at, LANES)] = (
+                d_values * (step_tokens * step_ref[3:4, 0:1])
+            ).astype(BF16)
+        d_q = both(*outs) * 0.125
         dqv_s[0, :, pl.ds(at, LANES)] += fold_rows(d_q)
         grad_s[step, :, pl.ds(at, LANES)] = (d_q * (step_tokens * step_ref[1:2, 0:1])).astype(BF16)
-        for n, (k0, k1, q0, q1) in enumerate(TILES):
-            grad_s[step, k0:k1, pl.ds(D + at, LANES)] = (
-                d_keys[n] * (step_tokens * step_ref[2:3, 0:1] * (1.0 / LOG2E))
-            ).astype(BF16)
-            dqv_s[1, :, pl.ds(at, LANES)] += fold_rows(d_values[n])
-            grad_s[step, k0:k1, pl.ds(2 * D + at, LANES)] = (
-                d_values[n] * (step_tokens * step_ref[3:4, 0:1])
-            ).astype(BF16)
         return carry
 
     @pl.when(step < rows)
@@ -991,28 +992,105 @@
             if now == ticks[len(ticks) // 3]:
                 vectors()
             if now == max(19, ended[0]):
-                dup_out[...] = passing(joined(0, 2), up_sh[...], step_ref[5:6, 0:1])
+                dup_out[...] = joined(0, 2)
             if now == max(19, ended[1]):
-                ddown_out[...] = passing(
-                    jnp.transpose(joined(1, 3).astype(F32)), down_sh[...], step_ref[6:7, 0:1]
-                )
+                ddown_out[...] = joined(1, 3)
             if now == max(19, ended[2]):
-                dproj = streams[4].out[...].reshape(-1, D)[:width]
-                dproj_out[...] = passing(dproj, proj_sh[...], step_ref[4:5, 0:1])
+                dproj_out[...] = streams[4].out[...].reshape(-1, D)[:width]
         whole = jnp.concatenate(
             [streams[5 + q].out[...].reshape(-1, D) for q in range(THIRDS)], axis=0
-        ).astype(F32)
-        for i in range(3):
-            dqkv_out[i] = passing(
-                jnp.transpose(whole[i * width : (i + 1) * width]),
-                qkv_sh[i],
-                step_ref[1 + i : 2 + i, 0:1],
-            )
+        )
+        dqkv_out[...] = whole[: 3 * width]
+
+
+def deliver_kernel(
+    step_ref,
+    tg_ref,
+    dqkv_ref,
+    dqv_ref,
+    dproj_ref,
+    dup_ref,
+    dub_ref,
+    ddown_ref,
+    vec_ref,
+    qkv_ref,
+    proj_ref,
+    up_ref,
+    down_ref,
+    tg_out,
+    dqkv_out,
+    dqv_out,
+    dproj_out,
+    dup_out,
+    dub_out,
+    ddown_out,
+    *vec_outs,
+):
+    width = dqkv_out.shape[-1]
+    tg_out[...] = tg_ref[...].astype(F32)
+    for i in range(3):
+        grad = jnp.transpose(dqkv_ref[i * width : (i + 1) * width].astype(F32))
+        dqkv_out[i] = passing(grad, qkv_ref[i], step_ref[1 + i : 2 + i, 0:1])
+    dproj_out[...] = passing(dproj_ref[...], proj_ref[...], step_ref[4:5, 0:1])
+    dup_out[...] = passing(dup_ref[...], up_ref[...], step_ref[5:6, 0:1])
+    grad = jnp.transpose(ddown_ref[...].astype(F32))
+    ddown_out[...] = passing(grad, down_ref[...], step_ref[6:7, 0:1])
+    dqv_out[...] = dqv_ref[...]
+    dub_out[...] = dub_ref[0]
+    for n, out in enumerate(vec_outs):
+        out[...] = vec_ref[n, 0]
+
+
+def deliver(steps, tokens_grad, dqkv, dqv, dproj, dup, dub, ddown, vec, qkv_w, proj_w, up_w, down_w):
+    rows = tokens_grad.shape[0] // SEQ
+    width, wide = qkv_w.shape[2], up_w.shape[1]
+
+    def whole(*shape):
+        return pl.BlockSpec(shape, lambda i: (0,) * len(shape))
+
+    def down_rows(*shape):
+        return pl.BlockSpec((shape[0] // rows,) + shape[1:], lambda i: (i, 0))
+
+    def along(*shape):
+        return pl.BlockSpec((shape[0], shape[1] // rows), lambda i: (0, i))
+
+    qkv_block = pl.BlockSpec((3, D // rows, width), lambda i: (0, i, 0))
+    outs = [
+        (tokens_grad.shape, down_rows(*tokens_grad.shape)),
+        (qkv_w.shape, qkv_block),
+        ((2, width), whole(2, width)),
+        (proj_w.shape, down_rows(*proj_w.shape)),
+        (up_w.shape, down_rows(*up_w.shape)),
+        ((wide,), whole(wide)),
+        (down_w.shape, down_rows(*down_w.shape)),
+    ] + [((D,), whole(D))] * 6
+    return pl.pallas_call(
+        deliver_kernel,
+        name="deliver",
+        grid=(rows,),
+        in_specs=[
+            whole(8, LANES),
+            down_rows(*tokens_grad.shape),
+            along(*dqkv.shape),
+            whole(2, width),
+            down_rows(*dproj.shape),
+            down_rows(*dup.shape),
+            whole(1, wide),
+            along(*ddown.shape),
+            whole(6, 1, D),
+            qkv_block,
+            down_rows(*proj_w.shape),
+            down_rows(*up_w.shape),
+            down_rows(*down_w.shape),
+        ],
+        out_specs=[spec for _, spec in outs],
+        out_shape=[jax.ShapeDtypeStruct(shape, F32) for shape, _ in outs],
+        compiler_params=pltpu.CompilerParams(vmem_limit_bytes=VMEM_LIMIT),
+    )(steps, tokens_grad, dqkv, dqv, dproj, dup, dub, ddown, vec, qkv_w, proj_w, up_w, down_w)
 
 
 def attend_back(
-    sizes, steps, tokens, ints, qkv, probs, ctx, gctx, first, qkv_full, dproj, dup, ddown, dub, dvec,
-    qkv_w, proj_w, up_w, down_w,
+    sizes, steps, tokens, ints, qkv, probs, ctx, gctx, first, qkv_full, dproj, dup, ddown, dub, dvec
 ):
     rows = tokens.shape[0] // SEQ
     parts, nz = 2 * sizes["x"], sizes["z"]
@@ -1028,12 +1106,12 @@
         return pl.BlockSpec(shape, lambda i: (0,) * len(shape))
 
     outs = [
-        ((3, D, width), F32),
+        ((3 * width, D), BF16),
         ((2, width), F32),
-        ((width, D), F32),
-        ((D, wide), F32),
+        ((width, D), BF16),
+        ((D, wide), BF16),
         ((1, wide), F32),
-        ((wide, D), F32),
+        ((D, wide), BF16),
         ((6, 1, D), F32),
     ]
     return pl.pallas_call(
@@ -1057,10 +1135,6 @@
             hbm,
             whole(*dub.shape),
             whole(*dvec.shape),
-            whole(*qkv_w.shape),
-            whole(*proj_w.shape),
-            whole(*up_w.shape),
-            whole(*down_w.shape),
         ],
         out_specs=[pl.BlockSpec((SEQ, D), late)] + [whole(*shape) for shape, _ in outs],
         scratch_shapes=[
@@ -1080,8 +1154,7 @@
             flops=rows * 6 * 10**9, bytes_accessed=rows * 8 * 10**6, transcendentals=0
         ),
     )(
-        steps, tokens, ints, qkv, probs, ctx, gctx, first, qkv_full, dproj, dup, ddown, dub, dvec,
-        qkv_w, proj_w, up_w, down_w,
+        steps, tokens, ints, qkv, probs, ctx, gctx, first, qkv_full, dproj, dup, ddown, dub, dvec
     )
 
 def local(
@@ -1120,13 +1193,15 @@
     layer_out, grad_first, grad_ctx, dproj, dup, ddown, dub, dvec = feed_forward(
         sizes, steps, biases, tokens, ctx, out_grad, proj_full.reshape(D, D), up_full, down_full, vecs
     )
-    tokens_grad, dqkv, dqv, dproj, dup, dub, ddown, vec = attend_back(
+    sums = attend_back(
         sizes, steps, tokens, ints, qkv, probs, ctx, grad_ctx, grad_first, qkv_full,
-        dproj, dup, ddown, dub, dvec, qkv_weight, proj_weight, up_weight, down_weight,
+        dproj, dup, ddown, dub, dvec,
     )
-    vec = [vec[n, 0] for n in range(6)]
+    tokens_grad, dqkv, dqv, dproj, dup, dub, ddown, *vec = deliver(
+        steps, *sums, qkv_weight, proj_weight, up_weight, down_weight
+    )
     return (
-        layer_out, tokens_grad.astype(F32), dqkv, dqv, dproj, vec[0], vec[1], vec[2], dup, dub[0], ddown,
+        layer_out, tokens_grad, dqkv, dqv, dproj, vec[0], vec[1], vec[2], dup, dub, ddown,
         vec[3], vec[4], vec[5],
     )
 

time: 201 us -> 186 us (0.925)
  Pallas kernels: 191 us -> 185 us
  local copies, waits for them, and re-layouts: 5.29 us -> 0 us
  other arithmetic: 4.28 us -> 0 us
    pallas_call x1, Pallas kernels: 86.9 us -> 79.5 us  [attend_back(): pl.pallas_call(lambda *refs: back_kernel(sizes, *refs), name='attend_back...]
    pallas_call x0 -> x1, Pallas kernels: none -> 6.32 us  [deliver(): pl.pallas_call(deliver_kernel, name='deliver', grid=(rows,), in_specs=[wh...]
    pallas_call x1, Pallas kernels: 59 us -> 54.1 us  [attend(): pl.pallas_call(lambda *refs: attend_kernel(sizes, *refs), name='attend',...]
    unnamed x20 -> x0, local copies, waits for them, and re-layouts: 4.69 us -> none
    convert_element_type x1 -> x0, other arithmetic: 4.28 us -> none  [local(): tokens_grad.astype(F32)]
where the time goes in v3:
time: 186 us
  Pallas kernels  185 us (99%)
    pallas_call x1, Pallas kernels, attend_back(): pl.pallas_call(lambda *refs: back_kernel(sizes, *refs), name='attend_back...  79.5 us
    pallas_call x1, Pallas kernels, attend(): pl.pallas_call(lambda *refs: attend_kernel(sizes, *refs), name='attend',...  54.1 us
    pallas_call x1, Pallas kernels, feed_forward(): pl.pallas_call(ffn_kernel, name='feed_forward', grid=(count // TB,), in_s...  45.1 us
    pallas_call x1, Pallas kernels, deliver(): pl.pallas_call(deliver_kernel, name='deliver', grid=(rows,), in_specs=[wh...  6.32 us

profile of v3, /device:TPU:0, one launch (start us, length us, event | category | flops | bytes accessed | tf_op | source)
XLA Modules:
  0.0 185.8 jit_solution(3752461672925492205)
XLA Ops:
  0.6 54.1 %attend.1 = (bf16[2048,512]{1,0:T(8,128)(2,1)}, bf16[2048,1536]{1,0:T(8,128)(2,1)}, bf16[4,8,2,256,384]{4,3,2,1,0:T(8,128)(2,1)}, bf16[2048,512]{1,0:T(8,128)(2,...) custom-call(s32[16]{0:T(128)} %refs_0_.1, ...), custom_call_target="tpu_custom_call" | custom-call | flops 12000000000 | bytes 24000000 | tf_op jit(solution)/shard_map/attend/pallas_call | solution.py:544
  54.7 45.1 %feed_forward.1 = (bf16[2048,512]{1,0:T(8,128)(2,1)}, f32[2048,512]{1,0:T(8,128)}, bf16[2048,512]{1,0:T(8,128)(2,1)}, bf16[4,2,4,16,512]{4,3,2,1,0:T(8,128)(2,1)...) custom-call(f32[8,128]{1,0:T(8,128)} %get-tuple-element.53.step_ref., ...), custom_call_target="tpu_custom_call" | custom-call | flops 28672000000 | bytes 24576000 | tf_op jit(solution)/shard_map/feed_forward/pallas_call | solution.py:749
  99.8 79.5 %attend_back.1 = (bf16[2048,512]{1,0:T(8,128)(2,1)}, bf16[384,512]{1,0:T(8,128)(2,1)}, f32[2,128]{1,0:T(2,128)}, bf16[128,512]{1,0:T(8,128)(2,1)}, bf16[512,512]...) custom-call(f32[8,128]{1,0:T(8,128)} %get-tuple-element.53.step_ref.refs_0_, ...), custom_call_target="tpu_custom_call" | custom-call | flops 24000000000 | bytes 32000000 | tf_op jit(solution)/shard_map/attend_back/pallas_call | solution.py:1117
  179.3 6.3 %deliver.1 = (f32[2048,512]{1,0:T(8,128)}, f32[3,512,128]{2,1,0:T(8,128)}, f32[2,128]{1,0:T(2,128)}, f32[128,512]{1,0:T(8,128)}, f32[512,512]{1,0:T(8,128)}, /*i...) custom-call(f32[8,128]{1,0:T(8,128)} %get-tuple-element.53.step_ref., ...), custom_call_target="tpu_custom_call" | custom-call | tf_op jit(solution)/shard_map/deliver/pallas_call | solution.py:1067

commit v4 on v3

--- a/solution.py
+++ b/solution.py
@@ -96,15 +96,34 @@
         return at[group], (at["z"] * 2 + at["y"], at["x"] * 2 + at["core"])
 
     def greet(self):
+        self.hello()
+        self.welcome()
+
+    def welcome(self, others=0):
+        count = sum(self.sizes[group] - 1 for group in MESH_AXES) + others
+        pl.semaphore_wait(pltpu.get_barrier_semaphore(), count)
+
+    def plane(self):
+        members = []
+        for k in range(self.sizes["x"]):
+            for side in range(2):
+                if k or side:
+                    at = dict(self.at)
+                    at["x"] = (at["x"] + k) % self.sizes["x"]
+                    at["y"] = (at["y"] + side) % 2
+                    device = (at["z"] * 2 + at["y"], at["x"] * 2 + at["core"])
+                    members.append((at["x"], at["y"], device))
+        return members
+
+    def hello(self, *others):
         barrier = pltpu.get_barrier_semaphore()
-        count = 0
+        for device in others:
+            pl.semaphore_signal(barrier, inc=1, device_id=device, device_id_type=MESH)
         for group in MESH_AXES:
             for k in range(1, self.sizes[group]):
                 pl.semaphore_signal(
                     barrier, inc=1, device_id=self.peer(group, k)[1], device_id_type=MESH
                 )
-                count += 1
-        pl.semaphore_wait(barrier, count)
 
 
 class Sems:
@@ -165,6 +184,14 @@
             return [
                 sems.copy(i, self.grad(2 * i + other), self.got_c.at[i], device) for i in range(nx)
             ]
+        if self.order == "plane":
+            if phase == 2:
+                return []
+            if phase == 1:
+                return [
+                    sems.copy(base + n, held.at[x, y], self.got_1.at[n], device)
+                    for n, (x, y, device) in enumerate(place.plane())
+                ]
         if phase == 1 and self.order == "xy":
             return exchange(
                 place, "x", lambda k, j: held.at[j], lambda k, j: self.got_1.at[k - 1], sems, base
@@ -221,10 +248,14 @@
                 held[at["x"], y] = add(
                     held[at["x"], y], *[self.got_1[k, y] for k in range(nx - 1)]
                 )
+        elif phase == 1 and self.order == "plane":
+            held[at["x"], at["y"]] = add(
+                held[at["x"], at["y"]], *[self.got_1[n] for n in range(2 * nx - 1)]
+            )
         elif phase == 1:
             for i in range(nx):
                 held[i, at["y"]] = add(held[i, at["y"]], self.got_1[i])
-        elif phase == 2:
+        elif phase == 2 and self.order != "plane":
             count = 1 if self.order == "xy" else nx - 1
             held[at["x"], at["y"]] = add(
                 held[at["x"], at["y"]], *[self.got_2[k] for k in range(count)]
@@ -239,8 +270,8 @@
     nx, nz = sizes["x"], sizes["z"]
     count = 3 * nx + 2 * nz + 1
     piece = (nz, rows, lanes)
-    first = (nx - 1, 2) if order == "xy" else (nx,)
-    second = (1,) if order == "xy" else (nx - 1,)
+    first = {"xy": (nx - 1, 2), "yx": (nx,), "plane": (2 * nx - 1,)}[order]
+    second = (nx - 1,) if order == "yx" else (1,)
     return [
         pltpu.VMEM((nx, 2) + piece, BF16),
         pltpu.VMEM((nx, 2) + piece, BF16),
@@ -339,8 +370,37 @@
         self.mine().wait()
 
 
+class SplitGather(Gather):
+    def far(self):
+        place, y = self.place, self.place.at["y"]
+        mine, half = self.every.at[place.part, y], self.own.at[y]
+        return exchange(place, "x", lambda k, j: half, lambda k, j: mine, self.sems, 0)
+
+    def side(self):
+        place = self.place
+        nx, y = place.size("x"), place.at["y"]
+        copies = []
+        for k in range(1, nx):
+            chip = (place.at["x"] + nx - k) % nx
+            half = self.every.at[chip * 2 + place.at["core"], y]
+            copies.append(self.sems.copy(2 * nx - 2 + k, half, half, place.peer("y", 1)[1]))
+        return copies
+
+    def cross(self):
+        for copy in self.far():
+            copy.wait()
+        for copy in self.side():
+            copy.start()
+
+    def forward(self):
+        for copy in self.side():
+            copy.wait()
+        for k in range(1, self.place.size("x")):
+            self.near(k).start()
+
+
 def gather_scratch(sizes):
-    count = 2 * sizes["x"] - 1
+    count = 3 * sizes["x"] - 2
     return [
         pltpu.SemaphoreType.DMA((count,)),
         pltpu.SemaphoreType.DMA((count,)),
@@ -398,6 +458,7 @@
     up_all,
     down_all,
     mask_s,
+    ints_s,
     raw_all,
     bias_all,
     bias_own,
@@ -416,15 +477,16 @@
         for n, (own, every) in enumerate(((qkv_sh, raw_all), (bias_own, bias_all)))
     ]
     late = [
-        Gather(place, own, every, *sems[6 + 3 * n : 9 + 3 * n])
+        SplitGather(place, own, every, *sems[6 + 3 * n : 9 + 3 * n])
         for n, (own, every) in enumerate(
-            ((up_own, up_all), (down_own, down_all), (proj_own, proj_all))
+            ((proj_own, proj_all), (up_own, up_all), (down_own, down_all))
         )
     ]
     peaks = Small(place, jnp.maximum, *sems[15:18])
 
     @pl.when(row == 0)
     def _():
+        place.hello()
         bias_own[...] = tile_rows(
             [ub_sh[...].astype(F32)[None], qvb_sh[0:1].astype(F32), qvb_sh[1:2].astype(F32)],
             8,
@@ -433,21 +495,26 @@
         tops = [top(tok_ref[...])] + [top(qkv_sh[i]) for i in range(3)]
         tops += [top(proj_sh[...]), top(up_sh[...]), top(down_sh[...])]
         total = tile_rows([jnp.broadcast_to(t, (1, LANES)) for t in tops], 8, LANES)
-        place.greet()
+        place.welcome()
         peaks.start(0, total)
         for gather in early:
             gather.start()
         peaks.start(1, peaks.finish(0))
         step_ref[...] = peaks.finish(1) / LEVELS
-        proj_own[...] = rounded(proj_sh[...].astype(F32) / step_ref[4:5, 0:1]).astype(BF16)
-        up_own[...] = rounded(up_sh[...].astype(F32) / step_ref[5:6, 0:1]).astype(BF16)
-        down_own[...] = rounded(down_sh[...].astype(F32) / step_ref[6:7, 0:1]).astype(BF16)
+        for own, shard, r in ((proj_own, proj_sh, 4), (up_own, up_sh, 5), (down_own, down_sh, 6)):
+            for h in range(2):
+                half = shard[h * own.shape[1] : (h + 1) * own.shape[1]]
+                own[h] = rounded(half.astype(F32) / step_ref[r : r + 1, 0:1]).astype(BF16)
+        for r in range(ints_s.shape[0] // SEQ):
+            rows = slice(r * SEQ, (r + 1) * SEQ)
+            ints_s[rows] = rounded(tok_ref[rows].astype(F32) / step_ref[0:1, 0:1]).astype(BF16)
+            if r == 0:
+                for gather in early:
+                    gather.forward()
+        for gather in early:
+            gather.finish()
         for gather in late:
             gather.start()
-        for gather in early:
-            gather.forward()
-        for gather in early:
-            gather.finish()
         bias_ref[...] = bias_all[...]
         for t in range(parts):
             for i in range(3):
@@ -455,14 +522,16 @@
                     raw_all[t, i].astype(F32) / step_ref[1 + i : 2 + i, 0:1]
                 ).astype(BF16)
 
+    for n, gather in enumerate(late):
+        pl.when(row == jnp.minimum((1, 1, 2)[n], last))(gather.cross)
+
     @pl.when(row == last)
     def _():
         for gather in late:
             gather.forward()
 
     step_tokens = step_ref[0:1, 0:1]
-    tok = tok_ref[pl.ds(pl.multiple_of(row * SEQ, SEQ), SEQ), :]
-    ints = rounded(tok.astype(F32) / step_tokens).astype(BF16)
+    ints = ints_s[pl.ds(pl.multiple_of(row * SEQ, SEQ), SEQ), :]
     ints_ref[...] = ints
     biases = [
         jnp.concatenate([bias_all[t, r : r + 1, :width] for t in range(parts)], axis=1)
@@ -536,7 +605,7 @@
     rows = tokens.shape[0] // SEQ
     parts = 2 * sizes["x"]
     hbm = pl.BlockSpec(memory_space=pl.ANY)
-    gathered = [(w.shape, BF16) for w in (proj_w, up_w, down_w)]
+    halves = [(2, w.shape[0] // 2, w.shape[1]) for w in (proj_w, up_w, down_w)]
 
     def whole(*shape):
         return pl.BlockSpec(shape, lambda i, *_: (0,) * len(shape))
@@ -572,11 +641,12 @@
             ],
             scratch_shapes=[
                 pltpu.VMEM((2, 256, 384), F32),
+                pltpu.VMEM(tokens.shape, BF16),
                 pltpu.VMEM((parts,) + qkv_w.shape, BF16),
                 pltpu.VMEM((parts, 8, up_b.shape[0]), F32),
                 pltpu.VMEM((8, up_b.shape[0]), F32),
             ]
-            + [pltpu.VMEM(w.shape, BF16) for w in (proj_w, up_w, down_w)]
+            + [pltpu.VMEM(shape, BF16) for shape in halves]
             + sum([gather_scratch(sizes) for _ in range(5)], [])
             + small_scratch(sizes, 8, LANES),
         ),
@@ -589,7 +659,7 @@
             jax.ShapeDtypeStruct((8, LANES), F32),
             jax.ShapeDtypeStruct((parts, 8, up_b.shape[0]), F32),
         ]
-        + [jax.ShapeDtypeStruct((parts,) + w.shape, BF16) for w in (proj_w, up_w, down_w)],
+        + [jax.ShapeDtypeStruct((parts,) + shape, BF16) for shape in halves],
         compiler_params=pltpu.CompilerParams(
             vmem_limit_bytes=VMEM_LIMIT, collective_id=0, has_side_effects=True
         ),
@@ -739,6 +809,7 @@
     count = tokens.shape[0]
     parts, nz = 2 * sizes["x"], sizes["z"]
     wide = FF // parts
+    proj, up, down = proj.reshape(D, D), up.reshape(parts, D, wide), down.reshape(parts, wide, D)
     split = (parts, 2, 2, nz, split_rows(D, 4 * nz), wide)
     split_proj = (parts, 2, nz, split_rows(D // parts, 2 * nz), D)
     block = pl.BlockSpec((TB, D), lambda i, *_: (i, 0))
@@ -798,16 +869,16 @@
 
 
 PLANS = (
-    ((0, 2), (2, 6), (7, 10), (10, 13), (13, 16), (16, 20)),
-    ((0, 2), (2, 6), (7, 10), (11, 14), (15, 19), (19, 22)),
-    ((0, 3), (4, 8), (8, 11), (12, 15), (16, 20), (21, 27)),
-    ((0, 3), (4, 8), (8, 11), (17, 21), (21, 25), (25, 33)),
-    ((0, 3), (9, 12), (12, 14), (19, 23), (23, 26), (29, 35)),
-    ((16, 19), (19, 22), (23, 29), (29, 32), (32, 37), (37, 40)),
-    ((16, 19), (19, 24), (24, 28), (28, 31), (31, 36), (36, 39)),
-    ((16, 19), (19, 24), (24, 30), (30, 34), (34, 38), (38, 41)),
+    ((0, 2), (2, 6), (6, 9), (9, 12), (12, 15), (15, 19)),
+    ((0, 2), (4, 8), (8, 11), (11, 14), (14, 17), (17, 21)),
+    ((0, 3), (6, 11), (11, 14), (14, 19), (19, 24), (24, 31)),
+    ((0, 3), (8, 13), (13, 16), (16, 20), (20, 26), (26, 34)),
+    ((0, 3), (11, 14), (14, 16), (17, 22), (23, 27), (29, 36)),
+    ((16, 19), (19, 23), (-1, -1), (24, 29), (29, 33), (33, 38)),
+    ((16, 19), (19, 25), (-1, -1), (25, 30), (30, 35), (35, 39)),
+    ((16, 19), (22, 28), (-1, -1), (28, 32), (32, 37), (37, 40)),
 )
-ORDERS = ('xy', 'yx', 'xy', 'yx', 'xy', 'xy', 'yx', 'xy')
+ORDERS = ('xy', 'xy', 'xy', 'xy', 'xy', 'plane', 'plane', 'plane')
 THIRDS = 3
 
 
@@ -870,7 +941,9 @@
     def _():
         dqkv_s[...] = jnp.zeros_like(dqkv_s)
         dqv_s[...] = jnp.zeros_like(dqv_s)
-        place.greet()
+        corners = [device for n, (_, _, device) in enumerate(place.plane()) if n > 1 and n % 2 == 0]
+        place.hello(*corners)
+        place.welcome(len(corners))
 
     def events(now):
         for s, plan in enumerate(PLANS):
@@ -1191,7 +1264,7 @@
     )
     vecs = (proj_bias, first_gain, first_shift, down_bias, second_gain, second_shift)
     layer_out, grad_first, grad_ctx, dproj, dup, ddown, dub, dvec = feed_forward(
-        sizes, steps, biases, tokens, ctx, out_grad, proj_full.reshape(D, D), up_full, down_full, vecs
+        sizes, steps, biases, tokens, ctx, out_grad, proj_full, up_full, down_full, vecs
     )
     sums = attend_back(
         sizes, steps, tokens, ints, qkv, probs, ctx, grad_ctx, grad_first, qkv_full,

time: 186 us -> 182 us (0.978)
  Pallas kernels: 185 us -> 181 us
    pallas_call x1, Pallas kernels: 54.1 us -> 51.5 us  [attend(): pl.pallas_call(lambda *refs: attend_kernel(sizes, *refs), name='attend',...]
where the time goes in v4:
time: 182 us
  Pallas kernels  181 us (99%)
    pallas_call x1, Pallas kernels, attend_back(): pl.pallas_call(lambda *refs: back_kernel(sizes, *refs), name='attend_back...  77.8 us
    pallas_call x1, Pallas kernels, attend(): pl.pallas_call(lambda *refs: attend_kernel(sizes, *refs), name='attend',...  51.5 us
    pallas_call x1, Pallas kernels, feed_forward(): pl.pallas_call(ffn_kernel, name='feed_forward', grid=(count // TB,), in_s...  45.1 us
    pallas_call x1, Pallas kernels, deliver(): pl.pallas_call(deliver_kernel, name='deliver', grid=(rows,), in_specs=[wh...  6.32 us

profile of v4, /device:TPU:0, one launch (start us, length us, event | category | flops | bytes accessed | tf_op | source)
XLA Modules:
  0.0 181.6 jit_solution(4719034673159334359)
XLA Ops:
  0.6 51.5 %attend.1 = (bf16[2048,512]{1,0:T(8,128)(2,1)}, bf16[2048,1536]{1,0:T(8,128)(2,1)}, bf16[4,8,2,256,384]{4,3,2,1,0:T(8,128)(2,1)}, bf16[2048,512]{1,0:T(8,128)(2,...) custom-call(s32[16]{0:T(128)} %refs_0_.1, ...), custom_call_target="tpu_custom_call" | custom-call | flops 12000000000 | bytes 24000000 | tf_op jit(solution)/shard_map/attend/pallas_call | solution.py:613
  52.2 45.1 %feed_forward.1 = (bf16[2048,512]{1,0:T(8,128)(2,1)}, f32[2048,512]{1,0:T(8,128)}, bf16[2048,512]{1,0:T(8,128)(2,1)}, bf16[4,2,4,16,512]{4,3,2,1,0:T(8,128)(2,1)...) custom-call(f32[8,128]{1,0:T(8,128)} %get-tuple-element.53.step_ref., ...), custom_call_target="tpu_custom_call" | custom-call | flops 28672000000 | bytes 24576000 | tf_op jit(solution)/shard_map/feed_forward/pallas_call | solution.py:820
  97.2 77.8 %attend_back.1 = (bf16[2048,512]{1,0:T(8,128)(2,1)}, bf16[384,512]{1,0:T(8,128)(2,1)}, f32[2,128]{1,0:T(2,128)}, bf16[128,512]{1,0:T(8,128)(2,1)}, bf16[512,512]...) custom-call(f32[8,128]{1,0:T(8,128)} %get-tuple-element.53.step_ref.refs_0_, ...), custom_call_target="tpu_custom_call" | custom-call | flops 24000000000 | bytes 32000000 | tf_op jit(solution)/shard_map/attend_back/pallas_call | solution.py:1190
  175.1 6.3 %deliver.1 = (f32[2048,512]{1,0:T(8,128)}, f32[3,512,128]{2,1,0:T(8,128)}, f32[2,128]{1,0:T(2,128)}, f32[128,512]{1,0:T(8,128)}, f32[512,512]{1,0:T(8,128)}, /*i...) custom-call(f32[8,128]{1,0:T(8,128)} %get-tuple-element.53.step_ref., ...), custom_call_target="tpu_custom_call" | custom-call | tf_op jit(solution)/shard_map/deliver/pallas_call | solution.py:1140

commit v5 on v4

--- a/solution.py
+++ b/solution.py
@@ -150,6 +150,8 @@
 
 
 def add(first, *others):
+    if len(others) == 1:
+        return first + others[0]
     total = first.astype(F32)
     for other in others:
         total = total + other.astype(F32)
@@ -439,13 +441,13 @@
 def attend_kernel(
     sizes,
     len_ref,
-    tok_ref,
+    tok_hbm,
     seg_ref,
-    qkv_sh,
+    qkv_hbm,
     qvb_sh,
-    proj_sh,
-    up_sh,
-    down_sh,
+    proj_hbm,
+    up_hbm,
+    down_hbm,
     ub_sh,
     ints_ref,
     qkv_ref,
@@ -459,6 +461,12 @@
     down_all,
     mask_s,
     ints_s,
+    tok_ref,
+    qkv_sh,
+    proj_sh,
+    up_sh,
+    down_sh,
+    load_s,
     raw_all,
     bias_all,
     bias_own,
@@ -487,6 +495,22 @@
     @pl.when(row == 0)
     def _():
         place.hello()
+        loads = [
+            pltpu.make_async_copy(source, target, load_s.at[n])
+            for n, (source, target) in enumerate(
+                (
+                    (tok_hbm, tok_ref),
+                    (qkv_hbm, qkv_sh),
+                    (proj_hbm, proj_sh),
+                    (up_hbm, up_sh),
+                    (down_hbm, down_sh),
+                )
+            )
+        ]
+        for load in loads:
+            load.start()
+        for load in loads:
+            load.wait()
         bias_own[...] = tile_rows(
             [ub_sh[...].astype(F32)[None], qvb_sh[0:1].astype(F32), qvb_sh[1:2].astype(F32)],
             8,
@@ -618,13 +642,13 @@
             grid=(rows,),
             in_specs=[
                 pl.BlockSpec(memory_space=pltpu.SMEM),
-                whole(*tokens.shape),
+                hbm,
                 whole(*segments.shape),
-                whole(*qkv_w.shape),
+                hbm,
                 whole(*qv_bias.shape),
-                whole(*proj_w.shape),
-                whole(*up_w.shape),
-                whole(*down_w.shape),
+                hbm,
+                hbm,
+                hbm,
                 whole(*up_b.shape),
             ],
             out_specs=[
@@ -642,6 +666,12 @@
             scratch_shapes=[
                 pltpu.VMEM((2, 256, 384), F32),
                 pltpu.VMEM(tokens.shape, BF16),
+                pltpu.VMEM(tokens.shape, BF16),
+                pltpu.VMEM(qkv_w.shape, BF16),
+                pltpu.VMEM(proj_w.shape, BF16),
+                pltpu.VMEM(up_w.shape, BF16),
+                pltpu.VMEM(down_w.shape, BF16),
+                pltpu.SemaphoreType.DMA((5,)),
                 pltpu.VMEM((parts,) + qkv_w.shape, BF16),
                 pltpu.VMEM((parts, 8, up_b.shape[0]), F32),
                 pltpu.VMEM((8, up_b.shape[0]), F32),
@@ -708,8 +738,8 @@
     ctx_ref,
     og_ref,
     proj_ref,
-    up_ref,
-    down_ref,
+    up_hbm,
+    down_hbm,
     pb_ref,
     fg_ref,
     fs_ref,
@@ -731,14 +761,24 @@
     ddown_s,
     dub_s,
     dvec_s,
+    up_ref,
+    down_ref,
+    load_s,
 ):
     at = pl.program_id(0)
     last = pl.num_programs(0) - 1
     parts = up_ref.shape[0]
     step_proj, step_up, step_down = [step_ref[r : r + 1, 0:1] for r in (4, 5, 6)]
 
+    loads = [
+        pltpu.make_async_copy(up_hbm, up_ref, load_s.at[0]),
+        pltpu.make_async_copy(down_hbm, down_ref, load_s.at[1]),
+    ]
+
     @pl.when(at == 0)
     def _():
+        for load in loads:
+            load.start()
         dproj_s[...] = jnp.zeros_like(dproj_s)
         dup_s[...] = jnp.zeros_like(dup_s)
         ddown_s[...] = jnp.zeros_like(ddown_s)
@@ -753,6 +793,12 @@
     n1, r1 = normalize(first_in)
     normed = n1 * first_gain + first_shift
     low = normed.astype(BF16)
+
+    @pl.when(at == 0)
+    def _():
+        for load in loads:
+            load.wait()
+
     branch = None
     pre = dot_nn(low, up_ref[0])
     for t in range(parts):
@@ -762,8 +808,11 @@
         act = act.astype(BF16)
         act_s[t] = act
         slope_s[t] = slope
-        term = dot_nn(act, down_ref[t])
-        branch = term if branch is None else branch + term
+        if t:
+            term = dot_nn(held, down_ref[t - 1])
+            branch = term if branch is None else branch + term
+        held = act
+    branch = branch + dot_nn(held, down_ref[parts - 1])
     second_in = normed + (branch * step_down + down_bias)
     n2, r2 = normalize(second_in)
     out_ref[...] = (n2 * second_gain + second_shift).astype(BF16)
@@ -828,8 +877,8 @@
             block,
             block,
             whole(D, D),
-            whole(parts, D, wide),
-            whole(parts, wide, D),
+            pl.BlockSpec(memory_space=pl.ANY),
+            pl.BlockSpec(memory_space=pl.ANY),
         ]
         + [whole(D)] * 6,
         out_specs=[
@@ -850,6 +899,9 @@
             pltpu.VMEM((parts, D, wide), F32),
             pltpu.VMEM((parts, 8, wide), F32),
             pltpu.VMEM((6, 8, D), F32),
+            pltpu.VMEM((parts, D, wide), BF16),
+            pltpu.VMEM((parts, wide, D), BF16),
+            pltpu.SemaphoreType.DMA((2,)),
         ],
         out_shape=[
             jax.ShapeDtypeStruct((count, D), BF16),
@@ -896,7 +948,7 @@
     ctx_ref,
     gctx_ref,
     first_ref,
-    w_ref,
+    w_hbm,
     dproj_hbm,
     dup_hbm,
     ddown_hbm,
@@ -914,6 +966,8 @@
     dqkv_s,
     dqv_s,
     part_s,
+    w_ref,
+    load_s,
     *scratch,
 ):
     step = pl.program_id(0)
@@ -937,8 +991,11 @@
         streams.append(Stream(place, ORDERS[n], source, *refs[:8], own))
     sums = Small(place, jnp.add, *scratch[9 * len(sources) :])
 
+    load = pltpu.make_async_copy(w_hbm, w_ref, load_s.at[0])
+
     @pl.when(step == 0)
     def _():
+        load.start()
         dqkv_s[...] = jnp.zeros_like(dqkv_s)
         dqv_s[...] = jnp.zeros_like(dqv_s)
         corners = [device for n, (_, _, device) in enumerate(place.plane()) if n > 1 and n % 2 == 0]
@@ -1006,6 +1063,8 @@
         for i in range(3):
             dqkv_s[i] += dot_tn(grad_s[step, :, i * D : (i + 1) * D], ints_ref[...])
 
+    pl.when(step == rows)(load.wait)
+
     @pl.when(step == rows)
     def _():
         for t in range(parts):
@@ -1202,7 +1261,7 @@
             pl.BlockSpec((SEQ, D), early),
             pl.BlockSpec((SEQ, D), early),
             pl.BlockSpec((SEQ, D), late),
-            whole(3, D, D),
+            hbm,
             hbm,
             hbm,
             hbm,
@@ -1215,6 +1274,8 @@
             pltpu.VMEM((3, D, D), F32),
             pltpu.VMEM((2, 8, D), F32),
             pltpu.VMEM(part, BF16),
+            pltpu.VMEM((3, D, D), BF16),
+            pltpu.SemaphoreType.DMA((1,)),
         ]
         + sum([stream_scratch(sizes, o, *p) for o, p in zip(ORDERS, pieces)], [])
         + small_scratch(sizes, 16, D),

time: 182 us -> 181 us (level)
  no operation moved by 1% of the time
where the time goes in v5:
time: 181 us
  Pallas kernels  180 us (99%)
    pallas_call x1, Pallas kernels, attend_back(): pl.pallas_call(lambda *refs: back_kernel(sizes, *refs), name='attend_back...  78.4 us
    pallas_call x1, Pallas kernels, attend(): pl.pallas_call(lambda *refs: attend_kernel(sizes, *refs), name='attend',...  50.3 us
    pallas_call x1, Pallas kernels, feed_forward(): pl.pallas_call(ffn_kernel, name='feed_forward', grid=(count // TB,), in_s...  45 us
    pallas_call x1, Pallas kernels, deliver(): pl.pallas_call(deliver_kernel, name='deliver', grid=(rows,), in_specs=[wh...  6.32 us

profile of v5, /device:TPU:0, one launch (start us, length us, event | category | flops | bytes accessed | tf_op | source)
XLA Modules:
  0.0 180.9 jit_solution(1131319487405720189)
XLA Ops:
  0.6 50.3 %attend.1 = (bf16[2048,512]{1,0:T(8,128)(2,1)}, bf16[2048,1536]{1,0:T(8,128)(2,1)}, bf16[4,8,2,256,384]{4,3,2,1,0:T(8,128)(2,1)}, bf16[2048,512]{1,0:T(8,128)(2,...) custom-call(s32[16]{0:T(128)} %refs_0_.1, ...), custom_call_target="tpu_custom_call" | custom-call | flops 12000000000 | bytes 24000000 | tf_op jit(solution)/shard_map/attend/pallas_call | solution.py:637
  50.9 45.0 %feed_forward.1 = (bf16[2048,512]{1,0:T(8,128)(2,1)}, f32[2048,512]{1,0:T(8,128)}, bf16[2048,512]{1,0:T(8,128)(2,1)}, bf16[4,2,4,16,512]{4,3,2,1,0:T(8,128)(2,1)...) custom-call(f32[8,128]{1,0:T(8,128)} %get-tuple-element.53.step_ref., ...), custom_call_target="tpu_custom_call" | custom-call | flops 28672000000 | bytes 24576000 | tf_op jit(solution)/shard_map/feed_forward/pallas_call | solution.py:869
  96.0 78.4 %attend_back.1 = (bf16[2048,512]{1,0:T(8,128)(2,1)}, bf16[384,512]{1,0:T(8,128)(2,1)}, f32[2,128]{1,0:T(2,128)}, bf16[128,512]{1,0:T(8,128)(2,1)}, bf16[512,512]...) custom-call(f32[8,128]{1,0:T(8,128)} %get-tuple-element.53.step_ref.refs_0_, ...), custom_call_target="tpu_custom_call" | custom-call | flops 24000000000 | bytes 32000000 | tf_op jit(solution)/shard_map/attend_back/pallas_call | solution.py:1249
  174.4 6.3 %deliver.1 = (f32[2048,512]{1,0:T(8,128)}, f32[3,512,128]{2,1,0:T(8,128)}, f32[2,128]{1,0:T(2,128)}, f32[128,512]{1,0:T(8,128)}, f32[512,512]{1,0:T(8,128)}, /*i...) custom-call(f32[8,128]{1,0:T(8,128)} %get-tuple-element.53.step_ref., ...), custom_call_target="tpu_custom_call" | custom-call | tf_op jit(solution)/shard_map/deliver/pallas_call | solution.py:1199

commit v6 on v5

--- a/solution.py
+++ b/solution.py
@@ -837,7 +837,7 @@
     dvec_s[2] += fold_rows(back)
     grad_first = norm_back(back * first_gain, n1, r1)
     dvec_s[0] += fold_rows(grad_first)
-    first_ref[...] = grad_first
+    first_ref[...] = grad_first.astype(BF16)
     grad_proj = (grad_first * step_proj).astype(BF16)
     dproj_s[...] += dot_tn(ctx, grad_proj)
     gctx_ref[...] = dot_nt(grad_proj, proj_ref[...]).astype(BF16)
@@ -905,7 +905,7 @@
         ],
         out_shape=[
             jax.ShapeDtypeStruct((count, D), BF16),
-            jax.ShapeDtypeStruct((count, D), F32),
+            jax.ShapeDtypeStruct((count, D), BF16),
             jax.ShapeDtypeStruct((count, D), BF16),
             jax.ShapeDtypeStruct(split_proj, BF16),
             jax.ShapeDtypeStruct(split, BF16),
@@ -1108,7 +1108,7 @@
         for i in range(3):
             term = dot_nt(grads[:, i * D : (i + 1) * D], w_ref[i])
             total = term if total is None else total + term
-        tg_ref[...] = (first_ref[...] + passing(total, tok_ref[...], step_tokens)).astype(BF16)
+        tg_ref[...] = (first_ref[...].astype(F32) + passing(total, tok_ref[...], step_tokens)).astype(BF16)
 
     def joined(*group):
         halves = [streams[n].out[...].reshape(D // 2, FF // parts) for n in group]
@@ -1174,7 +1174,7 @@
 
 
 def deliver(steps, tokens_grad, dqkv, dqv, dproj, dup, dub, ddown, vec, qkv_w, proj_w, up_w, down_w):
-    rows = tokens_grad.shape[0] // SEQ
+    rows = max(1, tokens_grad.shape[0] // SEQ // 2)
     width, wide = qkv_w.shape[2], up_w.shape[1]
 
     def whole(*shape):

time: 181 us -> 180 us (level)
  no operation moved by 1% of the time
where the time goes in v6:
time: 180 us
  Pallas kernels  179 us (99%)
    pallas_call x1, Pallas kernels, attend_back(): pl.pallas_call(lambda *refs: back_kernel(sizes, *refs), name='attend_back...  78.2 us
    pallas_call x1, Pallas kernels, attend(): pl.pallas_call(lambda *refs: attend_kernel(sizes, *refs), name='attend',...  50.3 us
    pallas_call x1, Pallas kernels, feed_forward(): pl.pallas_call(ffn_kernel, name='feed_forward', grid=(count // TB,), in_s...  44.8 us
    pallas_call x1, Pallas kernels, deliver(): pl.pallas_call(deliver_kernel, name='deliver', grid=(rows,), in_specs=[wh...  5.32 us

profile of v6, /device:TPU:0, one launch (start us, length us, event | category | flops | bytes accessed | tf_op | source)
XLA Modules:
  0.0 179.5 jit_solution(12426796878055293733)
XLA Ops:
  0.6 50.3 %attend.1 = (bf16[2048,512]{1,0:T(8,128)(2,1)}, bf16[2048,1536]{1,0:T(8,128)(2,1)}, bf16[4,8,2,256,384]{4,3,2,1,0:T(8,128)(2,1)}, bf16[2048,512]{1,0:T(8,128)(2,...) custom-call(s32[16]{0:T(128)} %refs_0_.1, ...), custom_call_target="tpu_custom_call" | custom-call | flops 12000000000 | bytes 24000000 | tf_op jit(solution)/shard_map/attend/pallas_call | solution.py:637
  50.9 44.8 %feed_forward.1 = (bf16[2048,512]{1,0:T(8,128)(2,1)}, bf16[2048,512]{1,0:T(8,128)(2,1)}, bf16[2048,512]{1,0:T(8,128)(2,1)}, bf16[4,2,4,16,512]{4,3,2,1,0:T(8,128...) custom-call(f32[8,128]{1,0:T(8,128)} %get-tuple-element.53.step_ref., ...), custom_call_target="tpu_custom_call" | custom-call | flops 28672000000 | bytes 24576000 | tf_op jit(solution)/shard_map/feed_forward/pallas_call | solution.py:869
  95.8 78.2 %attend_back.1 = (bf16[2048,512]{1,0:T(8,128)(2,1)}, bf16[384,512]{1,0:T(8,128)(2,1)}, f32[2,128]{1,0:T(2,128)}, bf16[128,512]{1,0:T(8,128)(2,1)}, bf16[512,512]...) custom-call(f32[8,128]{1,0:T(8,128)} %get-tuple-element.53.step_ref.refs_0_, ...), custom_call_target="tpu_custom_call" | custom-call | flops 24000000000 | bytes 32000000 | tf_op jit(solution)/shard_map/attend_back/pallas_call | solution.py:1249
  174.0 5.3 %deliver.1 = (f32[2048,512]{1,0:T(8,128)}, f32[3,512,128]{2,1,0:T(8,128)}, f32[2,128]{1,0:T(2,128)}, f32[128,512]{1,0:T(8,128)}, f32[512,512]{1,0:T(8,128)}, /*i...) custom-call(f32[8,128]{1,0:T(8,128)} %get-tuple-element.53.step_ref., ...), custom_call_target="tpu_custom_call" | custom-call | tf_op jit(solution)/shard_map/deliver/pallas_call | solution.py:1199

commit v7 on v6

--- a/solution.py
+++ b/solution.py
@@ -482,15 +482,17 @@
     width = D // parts
     early = [
         Gather(place, own, every, *sems[3 * n : 3 * n + 3])
-        for n, (own, every) in enumerate(((qkv_sh, raw_all), (bias_own, bias_all)))
+        for n, (own, every) in enumerate(
+            [(bias_own, bias_all)] + [(qkv_sh.at[i], raw_all.at[i]) for i in range(3)]
+        )
     ]
     late = [
-        SplitGather(place, own, every, *sems[6 + 3 * n : 9 + 3 * n])
+        SplitGather(place, own, every, *sems[12 + 3 * n : 15 + 3 * n])
         for n, (own, every) in enumerate(
             ((proj_own, proj_all), (up_own, up_all), (down_own, down_all))
         )
     ]
-    peaks = Small(place, jnp.maximum, *sems[15:18])
+    peaks = Small(place, jnp.maximum, *sems[21:24])
 
     @pl.when(row == 0)
     def _():
@@ -532,19 +534,20 @@
         for r in range(ints_s.shape[0] // SEQ):
             rows = slice(r * SEQ, (r + 1) * SEQ)
             ints_s[rows] = rounded(tok_ref[rows].astype(F32) / step_ref[0:1, 0:1]).astype(BF16)
-            if r == 0:
-                for gather in early:
-                    gather.forward()
-        for gather in early:
-            gather.finish()
+        for gather in early[:2]:
+            gather.forward()
+        for i in range(3):
+            if i < 2:
+                early[2 + i].forward()
+            early[1 + i].finish()
+            for t in range(parts):
+                w_ref[i, :, t * width : (t + 1) * width] = rounded(
+                    raw_all[i, t].astype(F32) / step_ref[1 + i : 2 + i, 0:1]
+                ).astype(BF16)
         for gather in late:
             gather.start()
+        early[0].finish()
         bias_ref[...] = bias_all[...]
-        for t in range(parts):
-            for i in range(3):
-                w_ref[i, :, t * width : (t + 1) * width] = rounded(
-                    raw_all[t, i].astype(F32) / step_ref[1 + i : 2 + i, 0:1]
-                ).astype(BF16)
 
     for n, gather in enumerate(late):
         pl.when(row == jnp.minimum((1, 1, 2)[n], last))(gather.cross)
@@ -672,12 +675,12 @@
                 pltpu.VMEM(up_w.shape, BF16),
                 pltpu.VMEM(down_w.shape, BF16),
                 pltpu.SemaphoreType.DMA((5,)),
-                pltpu.VMEM((parts,) + qkv_w.shape, BF16),
+                pltpu.VMEM((3, parts) + qkv_w.shape[1:], BF16),
                 pltpu.VMEM((parts, 8, up_b.shape[0]), F32),
                 pltpu.VMEM((8, up_b.shape[0]), F32),
             ]
             + [pltpu.VMEM(shape, BF16) for shape in halves]
-            + sum([gather_scratch(sizes) for _ in range(5)], [])
+            + sum([gather_scratch(sizes) for _ in range(7)], [])
             + small_scratch(sizes, 8, LANES),
         ),
         out_shape=[

time: 180 us -> 182 us (1.011)
  Pallas kernels: 179 us -> 181 us
where the time goes in v7:
time: 182 us; the launch traced here: 181 us
  Pallas kernels  181 us (99%)
    pallas_call x1, Pallas kernels, attend_back(): pl.pallas_call(lambda *refs: back_kernel(sizes, *refs), name='attend_back...  78.7 us
    pallas_call x1, Pallas kernels, attend(): pl.pallas_call(lambda *refs: attend_kernel(sizes, *refs), name='attend',...  51.7 us
    pallas_call x1, Pallas kernels, feed_forward(): pl.pallas_call(ffn_kernel, name='feed_forward', grid=(count // TB,), in_s...  44.8 us
    pallas_call x1, Pallas kernels, deliver(): pl.pallas_call(deliver_kernel, name='deliver', grid=(rows,), in_specs=[wh...  5.32 us

profile of v7, /device:TPU:0, one launch (start us, length us, event | category | flops | bytes accessed | tf_op | source)
XLA Modules:
  0.0 181.4 jit_solution(1313741678773651646)
XLA Ops:
  0.6 51.7 %attend.1 = (bf16[2048,512]{1,0:T(8,128)(2,1)}, bf16[2048,1536]{1,0:T(8,128)(2,1)}, bf16[4,8,2,256,384]{4,3,2,1,0:T(8,128)(2,1)}, bf16[2048,512]{1,0:T(8,128)(2,...) custom-call(s32[16]{0:T(128)} %refs_0_.1, ...), custom_call_target="tpu_custom_call" | custom-call | flops 12000000000 | bytes 24000000 | tf_op jit(solution)/shard_map/attend/pallas_call | solution.py:640
  52.4 44.8 %feed_forward.1 = (bf16[2048,512]{1,0:T(8,128)(2,1)}, bf16[2048,512]{1,0:T(8,128)(2,1)}, bf16[2048,512]{1,0:T(8,128)(2,1)}, bf16[4,2,4,16,512]{4,3,2,1,0:T(8,128...) custom-call(f32[8,128]{1,0:T(8,128)} %get-tuple-element.53.step_ref., ...), custom_call_target="tpu_custom_call" | custom-call | flops 28672000000 | bytes 24576000 | tf_op jit(solution)/shard_map/feed_forward/pallas_call | solution.py:872
  97.2 78.7 %attend_back.1 = (bf16[2048,512]{1,0:T(8,128)(2,1)}, bf16[384,512]{1,0:T(8,128)(2,1)}, f32[2,128]{1,0:T(2,128)}, bf16[128,512]{1,0:T(8,128)(2,1)}, bf16[512,512]...) custom-call(f32[8,128]{1,0:T(8,128)} %get-tuple-element.53.step_ref.refs_0_, ...), custom_call_target="tpu_custom_call" | custom-call | flops 24000000000 | bytes 32000000 | tf_op jit(solution)/shard_map/attend_back/pallas_call | solution.py:1252
  175.9 5.3 %deliver.1 = (f32[2048,512]{1,0:T(8,128)}, f32[3,512,128]{2,1,0:T(8,128)}, f32[2,128]{1,0:T(2,128)}, f32[128,512]{1,0:T(8,128)}, f32[512,512]{1,0:T(8,128)}, /*i...) custom-call(f32[8,128]{1,0:T(8,128)} %get-tuple-element.53.step_ref., ...), custom_call_target="tpu_custom_call" | custom-call | tf_op jit(solution)/shard_map/deliver/pallas_call | solution.py:1202
